TPU v7x, 256 devices: a whole 4x4x8 slice. The times are simulated.
256 devices in a mesh: gx: 16 (over y, x), gy: 4 (over z_hi, core), gz: 4 (over z_lo).
Axes of the slice: x: 4, y: 4, z: 8 (z_hi: 2, z_lo: 4; z = z_hi * 4 + z_lo), core: 2. Of those that a mesh axis runs over, the one named last changes fastest.
Arguments:
- coarse_density: float32 [64, 32, 256], P('gx', 'gy', 'gz'), may hold values from 0.02 to 2
- atom_count: int32 [16, 16], P('gx', ('gy', 'gz')), may hold values from 1 to 16, 128 in all within a row
- atom_species: int32 [16, 16, 16], P('gx', ('gy', 'gz')), may hold values from 0 to 1
- density_matrix: float32 [16, 16, 16, 324], P('gx', ('gy', 'gz')), as said below
- partial_waves: float32 [2, 18, 5000], replicated, may hold values from -1.8 to 1.8
- smooth_waves: float32 [2, 18, 5000], replicated, may hold values from -1.8 to 1.8
- core_density: float32 [2, 100], replicated, may hold values from 0.05 to 2
- smooth_core: float32 [2, 100], replicated, may hold values from 0.05 to 2
Outputs:
- potential: float32 [128, 64, 512], P('gx', 'gy', 'gz')
- energy_density: float32 [128, 64, 512], P('gx', 'gy', 'gz')
- atom_hamiltonian: float32 [16, 16, 16, 324], P('gx', ('gy', 'gz'))
- atom_energy: float32 [16, 16, 16], P('gx', ('gy', 'gz'))
Inputs may be any that keep to these rules, and one draw needn't show every extreme that they name: `atom_count`: the counts of the 16 domains that share one index of gx sum to 128, and in every such row the largest count is exactly 16. `density_matrix`: each slot holds a symmetric positive semidefinite 18 x 18 matrix.
All inputs are finite; a program needn't handle non-finite values.
Results may differ from a plain program's by a relative error of at most 0.0003.
Values sent between devices are 32-bit elements; how exact they have to be, the bound alone decides.
No kernel may reach another device: no remote copies, remote signals or barrier semaphores. Data moves between devices by JAX's collectives and lax.ppermute only.
A program may use at most 64 MiB of HBM per device.

v0:
```python
import functools
import math

import jax
import jax.numpy as jnp
import numpy as np
from jax import lax
from jax.experimental import pallas as pl
from jax.experimental.pallas import tpu as pltpu
from jax.sharding import PartitionSpec as P

fine_step = 0.1
sphere_radius = 2.5
enhance_kappa = 0.804
enhance_mu = 0.2195149727645171
gradient_beta = 0.06672455060314922
gradient_gamma = (1.0 - math.log(2.0)) / math.pi**2
perdew_amplitude = 0.031091
perdew_alpha = 0.2137
perdew_first = 7.5957
perdew_second = 3.5876
perdew_third = 1.6382
perdew_fourth = 0.49294

exchange_scale = -0.75 * (3.0 / math.pi) ** (1.0 / 3.0)
fermi_scale = (3.0 * math.pi**2) ** (1.0 / 3.0)
radius_scale = (3.0 / (4.0 * math.pi)) ** (1.0 / 3.0)
reduced_scale = 1.0 / (4.0 * fermi_scale**2)
scaled_scale = math.pi / (16.0 * fermi_scale)
beta_ratio = gradient_beta / gradient_gamma
fit = [
    2.0 * perdew_amplitude * c * radius_scale ** (k / 2.0)
    for k, c in ((1, perdew_first), (2, perdew_second), (3, perdew_third), (4, perdew_fourth))
]
ln2 = math.log(2.0)


def functional(n, s):
    m = jnp.exp2(jnp.log2(n) * (-1.0 / 6.0))
    m2 = m * m
    m4 = m2 * m2
    m8 = m4 * m4
    m14 = m8 * m4 * m2
    m16 = m8 * m8
    fitted = m * (fit[0] + m * (fit[1] + m * (fit[2] + m * fit[3])))
    slope = m * (fit[0] + m * (2.0 * fit[1] + m * (3.0 * fit[2] + m * (4.0 * fit[3]))))
    one_fit = 1.0 + fitted
    enhance = 1.0 + (enhance_mu / enhance_kappa * reduced_scale) * (s * m16)
    fit_both = fitted * one_fit
    joint = 1.0 / (fit_both * enhance)
    inverse_fit = joint * enhance
    damp = joint * fit_both
    log_term = jnp.log2(1.0 + one_fit * inverse_fit)
    alpha_r = (perdew_alpha * radius_scale) * m2
    one_alpha = 1.0 + alpha_r
    product_c = one_alpha * log_term
    c = (-2.0 * perdew_amplitude * ln2) * product_c
    inv_exp = 1.0 / (jnp.exp2((2.0 * perdew_amplitude / gradient_gamma) * product_c) - 1.0)
    c_n = (2.0 * perdew_amplitude / 3.0) * (
        ln2 * alpha_r * log_term - 0.5 * one_alpha * slope * inverse_fit
    )
    b = beta_ratio * inv_exp
    t = scaled_scale * (s * m14)
    q = b * t
    num = 1.0 + q
    den_inv = 1.0 / (1.0 + q * num)
    z = 1.0 + (beta_ratio * t) * (num * den_inv)
    z_inv = 1.0 / z
    h = (gradient_gamma * ln2) * jnp.log2(z)
    den_z = den_inv * z_inv
    h_t = gradient_beta * ((num + q) * den_inv) * den_z
    h_c = (t * (q * den_inv)) * ((q * (1.0 + num)) * den_z) * (b + beta_ratio)
    x = exchange_scale * (n * m4)
    xf = x * ((1.0 + enhance_kappa) - enhance_kappa * damp)
    damp2 = damp * damp
    xfp = (enhance_kappa * x) * (damp - damp2)
    e = n * (xf + c + h)
    e_n = (4.0 / 3.0) * xf - (8.0 / 3.0) * xfp + (c + h) + (1.0 - h_c) * c_n - (7.0 / 3.0) * (h_t * t)
    e_s = n * ((enhance_mu * reduced_scale) * (x * damp2 * m16) + scaled_scale * (h_t * m14))
    return e, e_n, e_s


ROW = 24


def radial_table(nrad, npts, width):
    g = np.arange(width) % nrad
    live = np.arange(width) < npts
    r = sphere_radius * (g + 0.5) / nrad
    w = r * r * (sphere_radius / nrad)
    k = nrad / sphere_radius
    up = np.where(g == nrad - 1, 0.0, np.where(g == 0, k, 0.5 * k))
    down = np.where(g == 0, 0.0, np.where(g == nrad - 1, -k, -0.5 * k))
    mid = np.where(g == 0, -k, np.where(g == nrad - 1, k, 0.0))
    rows = np.stack([w, up, mid, down] + [np.zeros(width)] * 4) * live
    return rows.astype(np.float32)


def atoms_kernel(
    ni, nrad, npts, na, width, chunk, sub,
    count_ref, species_ref, d_ref, ae_ref, ps_ref, ae_core_ref, ps_core_ref, radial_ref,
    h_ref, e_ref,
    lhs32, waves, packed, cores, rho, part_n, part_q, grads, total,
):
    f32, bf16 = jnp.float32, jnp.bfloat16
    tiles = width // 128
    row = lax.broadcasted_iota(jnp.int32, (na, 128), 0)
    species = jnp.zeros((na, 128), jnp.int32)
    for a in range(na):
        species = jnp.where(row == a, species_ref[0, 0, a], species)
    first = species == 0
    first_f = jnp.where(first, 1.0, 0.0).astype(f32)
    second_f = 1.0 - first_f

    lhs32[...] = jnp.zeros_like(lhs32)
    for i in range(ni):
        d = d_ref[:, ni * i : ni * (i + 1)]
        d1 = d.astype(bf16).astype(f32)
        d2 = d - d1
        here = pl.ds(na * i, na)
        for block, part in ((0, d1), (1, d1), (2, d2)):
            at = 2 * ROW * block
            lhs32[here, at : at + ni] = part * first_f[:, :ni]
            lhs32[here, at + ROW : at + ROW + ni] = part * second_f[:, :ni]

    cores[...] = jnp.zeros_like(cores)
    cores[0:2, 0:nrad] = ae_core_ref[...]
    cores[2:4, 0:nrad] = ps_core_ref[...]
    line = cores[...]
    lane = lax.broadcasted_iota(jnp.int32, (8, width), 1)
    reach = nrad
    while reach < width:
        line = jnp.where(lane < reach, line, pltpu.roll(line, reach, 1))
        reach *= 2
    cores[...] = line

    waves[...] = jnp.zeros_like(waves)
    e_total = jnp.zeros((na, 128), f32)
    rho[...] = jnp.ones_like(rho)
    part_q[...] = jnp.zeros_like(part_q)

    for table, x_ref in enumerate((ae_ref, ps_ref)):
        sign = 1.0 if table == 0 else -1.0
        scale = sign * 4.0 * math.pi * nrad / npts
        waves[0:ni, 0:npts] = x_ref[0]
        waves[ROW : ROW + ni, 0:npts] = x_ref[1]

        def wide_first(cols):
            return jnp.concatenate([first] * (cols // 128), axis=1)

        def density(k, _):
            at = pl.multiple_of(k * chunk, chunk)
            x = waves[:, pl.ds(at, chunk)]
            x1 = x.astype(bf16)
            x2 = (x - x1.astype(f32)).astype(bf16)
            right = jnp.concatenate([x1, x2, x1], axis=0)
            packed[0 : 4 * ROW, pl.ds(at, chunk)] = right[0 : 4 * ROW]
            mixed = jnp.dot(
                lhs32[:, 0 : 6 * ROW].astype(bf16), right, preferred_element_type=f32
            )
            pick = wide_first(chunk)
            value = jnp.where(
                pick,
                cores[2 * table : 2 * table + 1, pl.ds(at, chunk)],
                cores[2 * table + 1 : 2 * table + 2, pl.ds(at, chunk)],
            )
            for i in range(ni):
                own = jnp.where(pick, x[i : i + 1], x[ROW + i : ROW + i + 1])
                value = value + own * mixed[na * i : na * (i + 1)]
            rho[:, pl.ds(pl.multiple_of(at + 128, 128), chunk)] = value
            return 0

        lax.fori_loop(0, width // chunk, density, 0)

        def local(k, e_sum):
            at = pl.multiple_of(k * sub, sub)
            wide = rho[:, pl.ds(at, sub + 256)]
            n = wide[:, 128 : 128 + sub]
            after = pltpu.roll(wide, sub + 255, 1)[:, 128 : 128 + sub]
            before = pltpu.roll(wide, 1, 1)[:, 128 : 128 + sub]
            here = pl.ds(at, sub)
            weight = radial_ref[0:1, here]
            up, mid, down = radial_ref[1:2, here], radial_ref[2:3, here], radial_ref[3:4, here]
            slope = up * after + mid * n + down * before
            e, e_n, e_s = functional(n, slope * slope)
            weight = weight * scale
            we = e * weight
            for j in range(sub // 128):
                e_sum = e_sum + we[:, 128 * j : 128 * (j + 1)]
            part_n[:, here] = e_n * weight
            part_q[:, pl.ds(pl.multiple_of(at + 128, 128), sub)] = 2.0 * slope * e_s * weight
            return e_sum

        e_total = lax.fori_loop(0, width // sub, local, e_total)

        def back(k, _):
            at = pl.multiple_of(k * chunk, chunk)
            here = pl.ds(at, chunk)
            around = pl.ds(pl.multiple_of(at, 128), chunk + 256)
            wide = part_q[:, around]
            n_part = part_n[:, here]
            after = pltpu.roll(wide, chunk + 255, 1)[:, 128 : 128 + chunk]
            before = pltpu.roll(wide, 1, 1)[:, 128 : 128 + chunk]
            g = (
                n_part
                + radial_ref[5:6, here] * before
                + radial_ref[2:3, here] * wide[:, 128 : 128 + chunk]
                + radial_ref[6:7, here] * after
            )
            pick = wide_first(chunk)
            x = waves[:, here]
            for i in range(ni):
                own = jnp.where(pick, x[i : i + 1], x[ROW + i : ROW + i + 1]) * g
                hi = own.astype(bf16)
                grads[na * i : na * (i + 1), :] = hi
                grads[na * (ni + i) : na * (ni + i + 1), :] = (own - hi.astype(f32)).astype(bf16)
            out = lax.dot_general(
                grads[...], packed[0 : 4 * ROW, here], (((1,), (1,)), ((), ())),
                preferred_element_type=f32,
            )
            if table == 0:
                @pl.when(k == 0)
                def _():
                    total[...] = out

                @pl.when(k != 0)
                def _():
                    total[...] += out
            else:
                total[...] += out
            return 0

        lax.fori_loop(0, width // chunk, back, 0)

    tally = count_ref[0, 0]
    live = row < tally
    for i in range(ni):
        hi = total[na * i : na * (i + 1), :]
        lo = total[na * (ni + i) : na * (ni + i + 1), :]
        both = hi + lo
        value = both[:, 0 : 2 * ROW] + both[:, 2 * ROW : 4 * ROW]
        value = jnp.where(first[:, :ni], value[:, 0:ni], value[:, ROW : ROW + ni])
        h_ref[:, ni * i : ni * (i + 1)] = jnp.where(live[:, :ni], value, 0.0)
    energy = jnp.sum(e_total, axis=1, keepdims=True)
    energy = jnp.where(live[:, :1], energy, 0.0)
    diagonal = lax.broadcasted_iota(jnp.int32, (na, na), 0) == lax.broadcasted_iota(
        jnp.int32, (na, na), 1
    )
    e_ref[...] = jnp.sum(jnp.where(diagonal, energy, 0.0), axis=0, keepdims=True)


def atom_terms(count, species, matrices, ae, ps, ae_core, ps_core, chunk=2560, sub=1280):
    na, pairs = matrices.shape
    ni, npts = ae.shape[1], ae.shape[2]
    nrad = ae_core.shape[1]
    width = -(-npts // chunk) * chunk
    radial = radial_table(nrad, npts, width)
    radial[5] = np.roll(radial[1], 1)
    radial[6] = np.roll(radial[3], -1)
    vmem = pl.BlockSpec(memory_space=pltpu.VMEM)
    smem = pl.BlockSpec(memory_space=pltpu.SMEM)
    f32, bf16 = jnp.float32, jnp.bfloat16
    return pl.pallas_call(
        functools.partial(atoms_kernel, ni, nrad, npts, na, width, chunk, sub),
        out_shape=(
            jax.ShapeDtypeStruct((na, pairs), f32),
            jax.ShapeDtypeStruct((1, na), f32),
        ),
        in_specs=[smem, smem] + [vmem] * 6,
        out_specs=(vmem, vmem),
        scratch_shapes=[
            pltpu.VMEM((na * ni, 256), f32),
            pltpu.VMEM((2 * ROW, width), f32),
            pltpu.VMEM((4 * ROW, width), bf16),
            pltpu.VMEM((8, width), f32),
            pltpu.VMEM((na, width + 256), f32),
            pltpu.VMEM((na, width), f32),
            pltpu.VMEM((na, width + 256), f32),
            pltpu.VMEM((2 * na * ni, chunk), bf16),
            pltpu.VMEM((2 * na * ni, 4 * ROW), f32),
        ],
        compiler_params=pltpu.CompilerParams(vmem_limit_bytes=48 << 20),
        cost_estimate=pl.CostEstimate(
            flops=4 * na * ni * ni * npts * 2, transcendentals=na * npts * 10, bytes_accessed=3 << 20
        ),
        name="atoms",
    )(count, species, matrices, ae, ps, ae_core, ps_core, jnp.asarray(radial))


def with_halo(cells, sides, width):
    for axis, dim in sides:
        count = lax.axis_size(axis)
        even = lax.axis_index(axis) % 2 == 0
        head = lax.slice_in_dim(cells, 0, width, axis=dim)
        tail = lax.slice_in_dim(cells, cells.shape[dim] - width, cells.shape[dim], axis=dim)
        inner = [(i, i ^ 1) for i in range(count)]
        outer = [(i, (i + 1 if i % 2 else i - 1) % count) for i in range(count)]
        first = lax.ppermute(jnp.where(even, tail, head), axis, inner)
        second = lax.ppermute(jnp.where(even, head, tail), axis, outer)
        cells = jnp.concatenate(
            [jnp.where(even, second, first), cells, jnp.where(even, first, second)], axis=dim
        )
    return cells


def upsample_axis(values, direction):
    length = values.shape[direction]
    before_cell = lax.slice_in_dim(values, 0, length - 2, axis=direction)
    centre_cell = lax.slice_in_dim(values, 1, length - 1, axis=direction)
    after_cell = lax.slice_in_dim(values, 2, length, axis=direction)
    even_cells = 0.75 * centre_cell + 0.25 * before_cell
    odd_cells = 0.75 * centre_cell + 0.25 * after_cell
    paired = jnp.stack([even_cells, odd_cells], axis=direction + 1)
    new_shape = list(values.shape)
    new_shape[direction] = 2 * (length - 2)
    return paired.reshape(new_shape)


def upsample(values):
    for direction in range(3):
        values = upsample_axis(values, direction)
    return values


def grid_fields(extended):
    scale_back = 2.0 * fine_step
    interior = extended[1:-1, 1:-1, 1:-1]
    gradient = [
        (extended[2:, 1:-1, 1:-1] - extended[:-2, 1:-1, 1:-1]) / scale_back,
        (extended[1:-1, 2:, 1:-1] - extended[1:-1, :-2, 1:-1]) / scale_back,
        (extended[1:-1, 1:-1, 2:] - extended[1:-1, 1:-1, :-2]) / scale_back,
    ]
    sigma_field = gradient[0] * gradient[0] + gradient[1] * gradient[1] + gradient[2] * gradient[2]
    energy_values, by_density, by_sigma = functional(interior, sigma_field)
    flux_terms = [2.0 * by_sigma * gradient[direction] for direction in range(3)]
    divergence = (
        flux_terms[0][2:, 1:-1, 1:-1]
        - flux_terms[0][:-2, 1:-1, 1:-1]
        + (flux_terms[1][1:-1, 2:, 1:-1] - flux_terms[1][1:-1, :-2, 1:-1])
        + (flux_terms[2][1:-1, 1:-1, 2:] - flux_terms[2][1:-1, 1:-1, :-2])
    ) / scale_back
    return (by_density[1:-1, 1:-1, 1:-1] - divergence, energy_values[1:-1, 1:-1, 1:-1])


def shards(
    coarse_density,
    atom_count,
    atom_species,
    density_matrix,
    partial_waves,
    smooth_waves,
    core_density,
    smooth_core,
):
    rimmed = with_halo(coarse_density, (("gy", 1), ("gx", 0), ("gz", 2)), 2)
    fine = upsample(rimmed)
    potential, energy_density = grid_fields(fine)
    slot_total, pair_total = density_matrix.shape[2:]
    placed, placed_energy = atom_terms(
        atom_count,
        atom_species,
        density_matrix.reshape(slot_total, pair_total),
        partial_waves,
        smooth_waves,
        core_density,
        smooth_core,
    )
    return (
        potential,
        energy_density,
        placed.reshape(density_matrix.shape),
        placed_energy.reshape(atom_species.shape),
    )


def solution(mesh):
    in_specs = (
        P("gx", "gy", "gz"),
        P("gx", ("gy", "gz")),
        P("gx", ("gy", "gz"), None),
        P("gx", ("gy", "gz"), None, None),
        P(),
        P(),
        P(),
        P(),
    )
    out_specs = (
        P("gx", "gy", "gz"),
        P("gx", "gy", "gz"),
        P("gx", ("gy", "gz"), None, None),
        P("gx", ("gy", "gz"), None),
    )
    return jax.shard_map(shards, mesh=mesh, in_specs=in_specs, out_specs=out_specs, check_vma=False)
```

profile of v0, /device:TPU:1, one launch (start us, length us, event | category | flops | bytes accessed | tf_op | source)
XLA Modules:
  0.0 48.7 jit_solution(6480585200797498838)
XLA Ops:
  0.6 0.0 copy-start.9
  0.7 0.7 %copy-done.9 = f32[4,8,64]{2,1,0:T(8,128)S(1)} copy-done((f32[4,8,64]{2,1,0:T(8,128)S(1)}, f32[4,8,64]{2,1,0:T(8,128)}, u32[]{:S(2)}) %copy-start.9) | copy-done | bytes 8216
  1.4 8.3 %collective-permute-start = (f32[4,2,64]{2,1,0:T(2,128)S(1)}, f32[4,2,64]{2,1,0:T(2,128)S(1)}, u32[]{:S(2)}, u32[]{:S(2)}) collective-permute-start(f32[4,2,64]{2,1,0:T(2,128)S(1)} %get-tuple-element.58), channel_id=1, source_target_pairs={{0,12},{4,8},{8,4},{12,0},{1,13},{5,9},{9,5},{13,1},{2,14},{6,10},... | collective-permute-start | bytes 6152 | tf_op jit(solution)/shard_map/ppermute | solution.py:299
  9.7 0.0 collective-permute-start.1
  9.7 1.5 %collective-permute-done = f32[4,2,64]{2,1,0:T(2,128)S(1)} collective-permute-done((f32[4,2,64]{2,1,0:T(2,128)S(1)}, f32[4,2,64]{2,1,0:T(2,128)S(1)}, u32[]{:S(2)}, u32[]{:S(2)}) %collective-permute-start) | collective-permute-done | bytes 2080 | tf_op jit(solution)/shard_map/ppermute | solution.py:299
  11.1 0.0 collective-permute-done.1
  11.2 4.8 %collective-permute-start.2 = (f32[2,12,64]{2,1,0:T(8,128)S(1)}, f32[2,12,64]{2,1,0:T(8,128)S(1)}, u32[]{:S(2)}, u32[]{:S(2)}) collective-permute-start(f32[2,12,64]{2,1,0:T(8,128)S(1)} %get-tuple-element.56), channel_id=1, source_target_pairs={{0,240},{16,32},{32,16},{48,64},{64,48},{80,96},{96,80},{112,128},... | collective-permute-start | bytes 18440 | tf_op jit(solution)/shard_map/ppermute | solution.py:299
  16.0 0.0 collective-permute-start.3
  16.0 1.4 %copy.43.ae_ref = f32[2,18,5000]{2,1,0:T(8,128)S(1)} copy(f32[2,18,5000]{2,0,1:T(2,128)} %param.13) | data formatting | bytes 1440000 | tf_op args[4]
  17.4 0.0 copy-done.8
  17.5 0.2 copy.44.ps_ref
  18.3 0.0 collective-permute-done.2
  18.4 0.2 collective-permute-done.3
  18.6 0.0 copy-start
  18.6 0.0 copy-start.1
  18.6 0.1 slice_select_fusion.1
  18.7 2.9 %collective-permute-start.4 = (f32[8,12,2]{2,1,0:T(8,128)S(1)}, f32[8,12,2]{2,1,0:T(8,128)S(1)}, u32[]{:S(2)}, u32[]{:S(2)}) collective-permute-start(f32[8,12,2]{2,1,0:T(8,128)S(1)} %get-tuple-element.52), channel_id=1, source_target_pairs={{0,3},{1,2},{2,1},{3,0},{4,7},{5,6},{6,5},{7,4},{8,11},{9,10},{10,... | collective-permute-start | bytes 2312 | tf_op jit(solution)/shard_map/ppermute | solution.py:299
  21.7 0.0 collective-permute-start.5
  21.7 0.6 %copy-done.3 = f32[2,100]{1,0:T(2,128)S(1)} copy-done((f32[2,100]{1,0:T(2,128)S(1)}, f32[2,100]{1,0:T(2,128)}, u32[]{:S(2)}) %copy-start.3) | copy-done | bytes 824
  22.3 0.0 copy-done.2
  22.4 0.0 copy-done.4
  22.4 11.8 %atoms.1 = (f32[16,324]{1,0:T(8,128)}, f32[1,16]{1,0:T(1,128)}) custom-call(s32[1,1]{1,0:T(1,128)S(6)} %copy.52.count_ref, s32[1,1,16]{2,1,0:T(1,128)S(1)} %copy-done.4, f32[16,324]{1,0:T(8,128)S(1)} %bitcast.25, f32[2,18,5000]{2,1,0:T(8,128)S(1)} %copy.43.ae_ref, f32[2,18,5000]{2,1,0:T(8,128)S(1)} %copy.44.ps_ref, f32[2,100]{1,0:T(2,128)S(1)} %copy-done.2, ...), custom_call_target="tpu_custom_call" | custom-call | flops 207360000 | bytes 3145728 | tf_op jit(solution)/shard_map/atoms/pallas_call | solution.py:263
  34.2 0.0 collective-permute-done.4
  34.2 0.0 collective-permute-done.5
  34.2 0.1 pad_maximum_fusion.4
  34.3 0.1 copy.32
  34.4 0.1 reshape.26
  34.5 0.1 copy.34
  34.6 0.1 reshape.27
  34.7 0.1 fusion.26
  34.9 0.6 %copy.35 = f32[12,20,66,2]{1,3,2,0:T(2,128)S(1)} copy(f32[12,20,66,2]{2,1,0,3:T(8,128)S(1)} %pad_maximum_fusion) | data formatting | bytes 253440 | tf_op jit(solution)/shard_map/stack | solution.py:313
  35.5 0.6 %reshape.28 = f32[12,20,132]{1,2,0:T(8,128)S(1)} reshape(f32[12,20,66,2]{1,3,2,0:T(2,128)S(1)} %copy.35) | data formatting | bytes 253440 | tf_op jit(solution)/shard_map/reshape | solution.py:316
  36.0 2.7 %fusion.58 = (f32[10,18,130]{1,2,0:T(8,128)S(1)}, f32[10,18,130]{1,2,0:T(8,128)S(1)}, f32[10,18,130]{1,2,0:T(8,128)}, f32[10,18,130]{1,2,0:T(8,128)}, f32[10,18,...) fusion(f32[12,20,132]{1,2,0:T(8,128)S(1)} %reshape.28), kind=kLoop, calls=%fused_computation.119 | loop fusion | bytes 1310400 | tf_op jit(solution)/shard_map/slice | solution.py:330
  38.7 1.6 %copy.45 = f32[10,18,130]{2,1,0:T(8,128)S(1)} copy(f32[10,18,130]{1,2,0:T(8,128)} %get-tuple-element.32) | data formatting | bytes 187200
  40.3 0.4 copy.46
  40.7 2.3 %copy.47 = f32[10,18,130]{2,1,0:T(8,128)} copy(f32[10,18,130]{1,2,0:T(8,128)} %get-tuple-element.30) | data formatting | bytes 187200
  43.0 0.4 copy.48
  43.4 0.4 copy.49
  43.8 0.4 copy.50
  44.2 0.4 copy.51
  44.6 0.5 %copy-done.7 = f32[10,18,130]{2,1,0:T(8,128)S(1)} copy-done((f32[10,18,130]{2,1,0:T(8,128)S(1)}, f32[10,18,130]{2,1,0:T(8,128)}, u32[]{:S(2)}) %copy-start.7) | copy-done | bytes 93624
  45.2 0.4 subtract_multiply_fusion
  45.5 0.3 broadcast_multiply_fusion.1
  45.8 0.4 log_multiply_fusion
  46.2 0.5 %fusion.27 = (f32[10,18,130]{2,1,0:T(8,128)S(1)}, f32[10,18,130]{2,1,0:T(8,128)S(1)}, f32[10,18,130]{2,1,0:T(8,128)S(1)}, f32[10,18,130]{2,1,0:T(8,128)S(1)}, f3...) fusion(f32[10,18,130]{2,1,0:T(8,128)S(1)} %copy.46, ...), kind=kLoop, calls=%fused_computation.62 | loop fusion | flops 1310400 | bytes 1497600 | tf_op jit(solution)/shard_map/mul | solution.py:335
  46.7 0.1 fusion.28
  46.8 0.8 %slice_multiply_fusion.6 = f32[8,16,128]{2,1,0:T(8,128)} fusion(f32[10,18,130]{2,1,0:T(8,128)S(1)} %copy.45, f32[10,18,130]{2,1,0:T(8,128)S(1)} %get-tuple-element.21, f32[10,18,130]{2,1,0:T(8,128)S(1)} %get-tuple-element.19, f32[10,18,130]{2,1,0:T(8,128)S(1)} %get-tuple-element.16), kind=kLoop, calls=%fused_computation.72 | loop fusion | flops 49152 | bytes 327680 | tf_op jit(solution)/shard_map/mul | solution.py:77
  47.6 1.1 %fusion.36 = f32[8,16,128]{2,1,0:T(8,128)} fusion(f32[10,18,130]{2,1,0:T(8,128)S(1)} %get-tuple-element.43, f32[10,18,130]{2,1,0:T(8,128)S(1)} %get-tuple-element.42, f32[10,18,130]{2,1,0:T(8,128)S(1)} %get-tuple-element.24, f32[10,18,130]{2,1,0:T(8,128)S(1)} %get-tuple-element.41, f32[10,18,130]{2,1,0:T(8,128)S(1)} %get-tuple-element.26, ...), kind=kLoop, calls=%fused_computation.76 | loop fusion | flops 425984 | bytes 1376256 | tf_op jit(solution)/shard_map/sub | solution.py:342
  (23 shorter events, 0.2 us)
Async XLA Ops:
  0.6 0.7 %copy-start.9 = (f32[4,8,64]{2,1,0:T(8,128)S(1)}, f32[4,8,64]{2,1,0:T(8,128)}, u32[]{:S(2)}) copy-start(f32[4,8,64]{2,1,0:T(8,128)} %param.9) | copy-start | bytes 24580
  1.4 9.8 %collective-permute-start = (f32[4,2,64]{2,1,0:T(2,128)S(1)}, f32[4,2,64]{2,1,0:T(2,128)S(1)}, u32[]{:S(2)}, u32[]{:S(2)}) collective-permute-start(f32[4,2,64]{2,1,0:T(2,128)S(1)} %get-tuple-element.58), channel_id=1, source_target_pairs={{0,12},{4,8},{8,4},{12,0},{1,13},{5,9},{9,5},{13,1},{2,14},{6,10},... | collective-permute-start | bytes 6152 | tf_op jit(solution)/shard_map/ppermute | solution.py:299
  9.7 1.5 %collective-permute-start.1 = (f32[4,2,64]{2,1,0:T(2,128)S(1)}, f32[4,2,64]{2,1,0:T(2,128)S(1)}, u32[]{:S(2)}, u32[]{:S(2)}) collective-permute-start(f32[4,2,64]{2,1,0:T(2,128)S(1)} %get-tuple-element.59), channel_id=1, source_target_pairs={{0,4},{4,0},{8,12},{12,8},{1,5},{5,1},{9,13},{13,9},{2,6},{6,2},{1... | collective-permute-start | bytes 6152 | tf_op jit(solution)/shard_map/ppermute | solution.py:298
  11.2 7.2 %collective-permute-start.2 = (f32[2,12,64]{2,1,0:T(8,128)S(1)}, f32[2,12,64]{2,1,0:T(8,128)S(1)}, u32[]{:S(2)}, u32[]{:S(2)}) collective-permute-start(f32[2,12,64]{2,1,0:T(8,128)S(1)} %get-tuple-element.56), channel_id=1, source_target_pairs={{0,240},{16,32},{32,16},{48,64},{64,48},{80,96},{96,80},{112,128},... | collective-permute-start | bytes 18440 | tf_op jit(solution)/shard_map/ppermute | solution.py:299
  16.0 2.6 %collective-permute-start.3 = (f32[2,12,64]{2,1,0:T(8,128)S(1)}, f32[2,12,64]{2,1,0:T(8,128)S(1)}, u32[]{:S(2)}, u32[]{:S(2)}) collective-permute-start(f32[2,12,64]{2,1,0:T(8,128)S(1)} %get-tuple-element.57), channel_id=1, source_target_pairs={{0,16},{16,0},{32,48},{48,32},{64,80},{80,64},{96,112},{112,96},{1... | collective-permute-start | bytes 18440 | tf_op jit(solution)/shard_map/ppermute | solution.py:298
  16.0 1.4 %copy-start.8 = (f32[2,18,5000]{2,0,1:T(2,128)S(1)}, f32[2,18,5000]{2,0,1:T(2,128)}, u32[]{:S(2)}) copy-start(f32[2,18,5000]{2,0,1:T(2,128)} %param.14) | copy-start | bytes 2160004
  18.6 3.1 %copy-start = (f32[8,5120]{1,0:T(8,128)S(1)}, f32[8,5120]{1,0:T(8,128)}, u32[]{:S(2)}) copy-start(f32[8,5120]{1,0:T(8,128)} %constant.121.clone.radial_ref) | copy-start | bytes 491524
  18.6 3.1 %copy-start.1 = (f32[1,1,16,324]{3,2,1,0:T(8,128)S(1)}, f32[1,1,16,324]{3,2,1,0:T(8,128)}, u32[]{:S(2)}) copy-start(f32[1,1,16,324]{3,2,1,0:T(8,128)} %param.12) | copy-start | bytes 62212
  18.7 15.4 %collective-permute-start.4 = (f32[8,12,2]{2,1,0:T(8,128)S(1)}, f32[8,12,2]{2,1,0:T(8,128)S(1)}, u32[]{:S(2)}, u32[]{:S(2)}) collective-permute-start(f32[8,12,2]{2,1,0:T(8,128)S(1)} %get-tuple-element.52), channel_id=1, source_target_pairs={{0,3},{1,2},{2,1},{3,0},{4,7},{5,6},{6,5},{7,4},{8,11},{9,10},{10,... | collective-permute-start | bytes 2312 | tf_op jit(solution)/shard_map/ppermute | solution.py:299
  21.7 0.7 %copy-start.3 = (f32[2,100]{1,0:T(2,128)S(1)}, f32[2,100]{1,0:T(2,128)}, u32[]{:S(2)}) copy-start(f32[2,100]{1,0:T(2,128)} %ps_core_ref.1) | copy-start | bytes 2404
  21.7 0.7 %copy-start.2 = (f32[2,100]{1,0:T(2,128)S(1)}, f32[2,100]{1,0:T(2,128)}, u32[]{:S(2)}) copy-start(f32[2,100]{1,0:T(2,128)} %ae_core_ref.1) | copy-start | bytes 2404
  21.7 0.7 %copy-start.4 = (s32[1,1,16]{2,1,0:T(1,128)S(1)}, s32[1,1,16]{2,1,0:T(1,128)}, u32[]{:S(2)}) copy-start(s32[1,1,16]{2,1,0:T(1,128)} %species_ref.1) | copy-start | bytes 196
  21.7 12.5 %collective-permute-start.5 = (f32[8,12,2]{2,1,0:T(8,128)S(1)}, f32[8,12,2]{2,1,0:T(8,128)S(1)}, u32[]{:S(2)}, u32[]{:S(2)}) collective-permute-start(f32[8,12,2]{2,1,0:T(8,128)S(1)} %get-tuple-element.53), channel_id=1, source_target_pairs={{0,1},{1,0},{2,3},{3,2},{4,5},{5,4},{6,7},{7,6},{8,9},{9,8},{10,11... | collective-permute-start | bytes 2312 | tf_op jit(solution)/shard_map/ppermute | solution.py:298
  38.7 1.6 %copy-start.6 = (f32[10,18,130]{1,2,0:T(8,128)S(1)}, f32[10,18,130]{1,2,0:T(8,128)}, u32[]{:S(2)}) copy-start(f32[10,18,130]{1,2,0:T(8,128)} %get-tuple-element.31) | copy-start | bytes 280804
  40.7 2.3 %copy-start.5 = (f32[10,18,130]{1,2,0:T(8,128)S(1)}, f32[10,18,130]{1,2,0:T(8,128)}, u32[]{:S(2)}) copy-start(f32[10,18,130]{1,2,0:T(8,128)} %get-tuple-element.29) | copy-start | bytes 280804
  44.2 1.0 %copy-start.7 = (f32[10,18,130]{2,1,0:T(8,128)S(1)}, f32[10,18,130]{2,1,0:T(8,128)}, u32[]{:S(2)}) copy-start(f32[10,18,130]{2,1,0:T(8,128)} %copy.47) | copy-start | bytes 280804
where the time goes:
time: 49 us; the launch traced here: 48.7 us
  starting transfers between devices  16 us (33%)
  local copies, waits for them, and re-layouts  13.6 us (28%)
  Pallas kernels  11.8 us (24%)
  other arithmetic  4 us (8%)
  waiting for transfers between devices  1.73 us (4%)
  between operations  1.53 us (3%)
    ppermute x3, starting transfers between devices, with_halo(): second = lax.ppermute(jnp.where(even, head, tail), axis, outer)  16 us
    pallas_call x1, Pallas kernels, atom_terms(): pl.pallas_call(functools.partial(atoms_kernel, ni, nrad, npts, na, width,...  11.8 us
    unnamed x29, local copies, waits for them, and re-layouts  9.49 us
    slice x1, local copies, waits for them, and re-layouts, grid_fields(): extended[1:-1, :-2, 1:-1]  2.67 us
    ppermute x3, waiting for transfers between devices, with_halo(): second = lax.ppermute(jnp.where(even, head, tail), axis, outer)  1.49 us
    sub x1, other arithmetic, grid_fields(): by_density[1:-1, 1:-1, 1:-1] - divergence  1.07 us
  transfers between devices with their start and end apart: 6, of which 2 were waited for; matrix products, arithmetic and copies ran while one was open for 3% of the time, Pallas kernels for 24%

commit v1 on v0

--- a/solution.py
+++ b/solution.py
@@ -287,6 +287,107 @@
     )(count, species, matrices, ae, ps, ae_core, ps_core, jnp.asarray(radial))
 
 
+def upsampling(cells, halo):
+    table = np.zeros((2 * cells + 4, cells + 2 * halo))
+    for k in range(-2, 2 * cells + 2):
+        i = k // 2
+        table[k + 2, i + halo] = 0.75
+        table[k + 2, i + halo + (1 if k % 2 else -1)] = 0.25
+    return table
+
+
+def grid_tables(nx, ny, nz):
+    ux, uy, uz = upsampling(nx, 2), upsampling(ny, 2), upsampling(nz, 2)
+    fx, fy, fz = 2 * nx, 2 * ny, 2 * nz
+
+    def diff(u):
+        return np.concatenate([np.zeros_like(u[:1]), u[2:] - u[:-2], np.zeros_like(u[:1])])
+
+    places = [(-1, y) for y in range(fy)]
+    places += [(x, y) for x in range(fx) for y in range(fy)]
+    places += [(fx, y) for y in range(fy)]
+    places += [(x, -1) for x in range(fx)] + [(x, fy) for x in range(fx)]
+
+    def rows(wx, wy):
+        return np.stack([np.outer(wy[y + 2], wx[x + 2]).reshape(-1) for x, y in places])
+
+    left = np.concatenate([rows(ux, uy), rows(diff(ux), uy), rows(ux, diff(uy))])
+    beyond = np.array([fz] + [fz // 2] * (fz - 2) + [-1])
+    right = np.concatenate(
+        [w[at + 2] for w in (uz, diff(uz)) for at in (np.arange(fz), beyond)]
+    ).T
+    return np.concatenate([left] * 3, axis=1), right
+
+
+def split3(x):
+    f32, bf16 = jnp.float32, jnp.bfloat16
+    x1 = x.astype(bf16)
+    rest = x - x1.astype(f32)
+    x2 = rest.astype(bf16)
+    return x1, x2, (rest - x2.astype(f32)).astype(bf16)
+
+
+def grid_kernel(fx, fy, fz, c_ref, left_ref, right_ref, v_ref, e_ref):
+    f32 = jnp.float32
+    right = right_ref[...]
+    parts = [jnp.dot(p, right, preferred_element_type=f32) for p in split3(c_ref[...])]
+    lines = parts[0] + (parts[1] + parts[2])
+    stack = jnp.concatenate(split3(lines), axis=0)
+    inner = fx * fy
+    rows = inner + 2 * fy + 2 * fx
+    plane = jnp.dot(left_ref[...], stack[:, : 2 * fz], preferred_element_type=f32)
+    dz_all = jnp.dot(left_ref[0:rows, :], stack[:, 2 * fz :], preferred_element_type=f32)
+    inv = 0.5 / fine_step
+
+    def fields(lo, hi, tile):
+        cols = slice(fz * tile, fz * (tile + 1))
+        n, dx, dy = (plane[rows * k + lo : rows * k + hi, cols] for k in range(3))
+        dz = dz_all[lo:hi, cols]
+        s = (inv * inv) * (dx * dx + dy * dy + dz * dz)
+        return functional(n, s), dx, dy, dz
+
+    main = slice(fy, fy + inner)
+    (e, e_n, e_s), dx, dy, dz = fields(fy, fy + inner, 0)
+    e_ref[...] = e.reshape(fx, fy, fz)
+    (_, _, s_low), dx_low, _, _ = fields(0, fy, 0)
+    (_, _, s_high), dx_high, _, _ = fields(fy + inner, 2 * fy + inner, 0)
+    (_, _, s_side), _, dy_side, _ = fields(2 * fy + inner, rows, 0)
+    (_, _, s_end), _, _, dz_end = fields(fy, fy + inner, 1)
+    flux_x = jnp.concatenate([s_low * dx_low, e_s * dx, s_high * dx_high], axis=0)
+    change = flux_x[2 * fy :] - flux_x[: inner]
+    flux_z, end_z = e_s * dz, s_end * dz_end
+    lane = lax.broadcasted_iota(jnp.int32, (inner, fz), 1)
+    after = pltpu.roll(jnp.where(lane == 0, end_z, flux_z), fz - 1, 1)
+    before = pltpu.roll(jnp.where(lane == fz - 1, end_z, flux_z), 1, 1)
+    change = change + (after - before)
+    flux_y, side_y = e_s * dy, s_side * dy_side
+    line = lax.broadcasted_iota(jnp.int32, (fy, fz), 0)
+    for x in range(fx):
+        here = slice(fy * x, fy * (x + 1))
+        own = flux_y[here]
+        after = jnp.where(line == fy - 1, side_y[fx + x : fx + x + 1], pltpu.roll(own, fy - 1, 0))
+        before = jnp.where(line == 0, side_y[x : x + 1], pltpu.roll(own, 1, 0))
+        v_ref[x] = e_n[here] - (2.0 * inv * inv) * (change[here] + (after - before))
+
+
+def grid_terms(columns, nx, ny, nz):
+    left, right = grid_tables(nx, ny, nz)
+    fx, fy, fz = 2 * nx, 2 * ny, 2 * nz
+    vmem = pl.BlockSpec(memory_space=pltpu.VMEM)
+    fine = jax.ShapeDtypeStruct((fx, fy, fz), jnp.float32)
+    return pl.pallas_call(
+        functools.partial(grid_kernel, fx, fy, fz),
+        out_shape=(fine, fine),
+        in_specs=[vmem] * 3,
+        out_specs=(vmem, vmem),
+        compiler_params=pltpu.CompilerParams(vmem_limit_bytes=32 << 20),
+        cost_estimate=pl.CostEstimate(
+            flops=300 * fx * fy * fz, transcendentals=10 * fx * fy * fz, bytes_accessed=2 << 20
+        ),
+        name="grid",
+    )(columns, jnp.asarray(left, jnp.bfloat16), jnp.asarray(right, jnp.bfloat16))
+
+
 def with_halo(cells, sides, width):
     for axis, dim in sides:
         count = lax.axis_size(axis)
@@ -303,45 +404,6 @@
     return cells
 
 
-def upsample_axis(values, direction):
-    length = values.shape[direction]
-    before_cell = lax.slice_in_dim(values, 0, length - 2, axis=direction)
-    centre_cell = lax.slice_in_dim(values, 1, length - 1, axis=direction)
-    after_cell = lax.slice_in_dim(values, 2, length, axis=direction)
-    even_cells = 0.75 * centre_cell + 0.25 * before_cell
-    odd_cells = 0.75 * centre_cell + 0.25 * after_cell
-    paired = jnp.stack([even_cells, odd_cells], axis=direction + 1)
-    new_shape = list(values.shape)
-    new_shape[direction] = 2 * (length - 2)
-    return paired.reshape(new_shape)
-
-
-def upsample(values):
-    for direction in range(3):
-        values = upsample_axis(values, direction)
-    return values
-
-
-def grid_fields(extended):
-    scale_back = 2.0 * fine_step
-    interior = extended[1:-1, 1:-1, 1:-1]
-    gradient = [
-        (extended[2:, 1:-1, 1:-1] - extended[:-2, 1:-1, 1:-1]) / scale_back,
-        (extended[1:-1, 2:, 1:-1] - extended[1:-1, :-2, 1:-1]) / scale_back,
-        (extended[1:-1, 1:-1, 2:] - extended[1:-1, 1:-1, :-2]) / scale_back,
-    ]
-    sigma_field = gradient[0] * gradient[0] + gradient[1] * gradient[1] + gradient[2] * gradient[2]
-    energy_values, by_density, by_sigma = functional(interior, sigma_field)
-    flux_terms = [2.0 * by_sigma * gradient[direction] for direction in range(3)]
-    divergence = (
-        flux_terms[0][2:, 1:-1, 1:-1]
-        - flux_terms[0][:-2, 1:-1, 1:-1]
-        + (flux_terms[1][1:-1, 2:, 1:-1] - flux_terms[1][1:-1, :-2, 1:-1])
-        + (flux_terms[2][1:-1, 1:-1, 2:] - flux_terms[2][1:-1, 1:-1, :-2])
-    ) / scale_back
-    return (by_density[1:-1, 1:-1, 1:-1] - divergence, energy_values[1:-1, 1:-1, 1:-1])
-
-
 def shards(
     coarse_density,
     atom_count,
@@ -353,8 +415,8 @@
     smooth_core,
 ):
     rimmed = with_halo(coarse_density, (("gy", 1), ("gx", 0), ("gz", 2)), 2)
-    fine = upsample(rimmed)
-    potential, energy_density = grid_fields(fine)
+    columns = rimmed.transpose(1, 0, 2).reshape(-1, rimmed.shape[2])
+    potential, energy_density = grid_terms(columns, *coarse_density.shape)
     slot_total, pair_total = density_matrix.shape[2:]
     placed, placed_energy = atom_terms(
         atom_count,

time: 49 us -> 37.2 us (0.76)
  local copies, waits for them, and re-layouts: 13.6 us -> 3.96 us
  other arithmetic: 4 us -> 0.26 us
  Pallas kernels: 11.8 us -> 13.5 us
    unnamed x29 -> x20, local copies, waits for them, and re-layouts: 9.49 us -> 3.94 us
    slice x1 -> x0, local copies, waits for them, and re-layouts: 2.67 us -> none  [grid_fields(): extended[1:-1, :-2, 1:-1]]
    mul x6 -> x0, other arithmetic: 2.45 us -> none  [the longest x1 0.78 us: functional(): e = n * (xf + c + h)]
    pallas_call x0 -> x1, Pallas kernels: none -> 1.67 us  [grid_terms(): pl.pallas_call(functools.partial(grid_kernel, fx, fy, fz), out_shape=(fin...]
    sub x1 -> x0, other arithmetic: 1.07 us -> none  [grid_fields(): by_density[1:-1, 1:-1, 1:-1] - divergence]
    another operation x3 -> x0, local copies, waits for them, and re-layouts: 0.73 us -> none  [upsample_axis(): paired = jnp.stack([even_cells, odd_cells], axis=direction + 1)]
    reshape x3 -> x0, local copies, waits for them, and re-layouts: 0.7 us -> none  [upsample_axis(): return paired.reshape(new_shape)]
  transfers between devices with their start and end apart: 6 -> 6, of which waited for: 2 -> 2; matrix products, arithmetic and copies ran while one was open for 3% -> 5% of each run, Pallas kernels for 24% -> 32%
where the time goes in v1:
time: 37.2 us; the launch traced here: 36.9 us
  starting transfers between devices  16 us (43%)
  Pallas kernels  13.5 us (36%)
  local copies, waits for them, and re-layouts  3.96 us (11%)
  waiting for transfers between devices  1.71 us (5%)
  between operations  1.45 us (4%)
    ppermute x3, starting transfers between devices, with_halo(): second = lax.ppermute(jnp.where(even, head, tail), axis, outer)  16 us
    pallas_call x1, Pallas kernels, atom_terms(): pl.pallas_call(functools.partial(atoms_kernel, ni, nrad, npts, na, width,...  11.8 us
    unnamed x20, local copies, waits for them, and re-layouts  3.94 us
    pallas_call x1, Pallas kernels, grid_terms(): pl.pallas_call(functools.partial(grid_kernel, fx, fy, fz), out_shape=(fin...  1.67 us
    ppermute x3, waiting for transfers between devices, with_halo(): second = lax.ppermute(jnp.where(even, head, tail), axis, outer)  1.49 us
  transfers between devices with their start and end apart: 6, of which 2 were waited for; matrix products, arithmetic and copies ran while one was open for 5% of the time, Pallas kernels for 32%

profile of v1, /device:TPU:1, one launch (start us, length us, event | category | flops | bytes accessed | tf_op | source)
XLA Modules:
  0.0 36.9 jit_solution(17412958871656273885)
XLA Ops:
  0.6 0.0 copy-start.8
  0.7 0.7 %copy-done.8 = f32[4,8,64]{2,1,0:T(8,128)S(1)} copy-done((f32[4,8,64]{2,1,0:T(8,128)S(1)}, f32[4,8,64]{2,1,0:T(8,128)}, u32[]{:S(2)}) %copy-start.8) | copy-done | bytes 8216
  1.4 8.3 %collective-permute-start = (f32[4,2,64]{2,1,0:T(2,128)S(1)}, f32[4,2,64]{2,1,0:T(2,128)S(1)}, u32[]{:S(2)}, u32[]{:S(2)}) collective-permute-start(f32[4,2,64]{2,1,0:T(2,128)S(1)} %get-tuple-element.20), channel_id=1, source_target_pairs={{0,12},{4,8},{8,4},{12,0},{1,13},{5,9},{9,5},{13,1},{2,14},{6,10},... | collective-permute-start | bytes 6152 | tf_op jit(solution)/shard_map/ppermute | solution.py:400
  9.7 0.0 collective-permute-start.1
  9.7 1.5 %collective-permute-done = f32[4,2,64]{2,1,0:T(2,128)S(1)} collective-permute-done((f32[4,2,64]{2,1,0:T(2,128)S(1)}, f32[4,2,64]{2,1,0:T(2,128)S(1)}, u32[]{:S(2)}, u32[]{:S(2)}) %collective-permute-start) | collective-permute-done | bytes 2080 | tf_op jit(solution)/shard_map/ppermute | solution.py:400
  11.1 0.0 collective-permute-done.1
  11.2 4.8 %collective-permute-start.2 = (f32[2,12,64]{2,1,0:T(8,128)S(1)}, f32[2,12,64]{2,1,0:T(8,128)S(1)}, u32[]{:S(2)}, u32[]{:S(2)}) collective-permute-start(f32[2,12,64]{2,1,0:T(8,128)S(1)} %get-tuple-element.18), channel_id=1, source_target_pairs={{0,240},{16,32},{32,16},{48,64},{64,48},{80,96},{96,80},{112,128},... | collective-permute-start | bytes 18440 | tf_op jit(solution)/shard_map/ppermute | solution.py:400
  16.0 0.0 collective-permute-start.3
  16.7 0.0 copy-start.7
  16.7 1.4 %copy.16.ae_ref = f32[2,18,5000]{2,1,0:T(8,128)S(1)} copy(f32[2,18,5000]{2,0,1:T(2,128)} %param.15) | data formatting | bytes 1440000 | tf_op args[4]
  18.1 0.0 copy-done.7
  18.1 0.2 copy.17.ps_ref
  18.4 0.0 collective-permute-done.2
  18.4 0.2 collective-permute-done.3
  18.6 0.0 copy-start.1
  18.6 0.0 copy-start.3
  18.6 0.1 slice_select_fusion.1
  18.7 2.9 %collective-permute-start.4 = (f32[8,12,2]{2,1,0:T(8,128)S(1)}, f32[8,12,2]{2,1,0:T(8,128)S(1)}, u32[]{:S(2)}, u32[]{:S(2)}) collective-permute-start(f32[8,12,2]{2,1,0:T(8,128)S(1)} %get-tuple-element.14), channel_id=1, source_target_pairs={{0,3},{1,2},{2,1},{3,0},{4,7},{5,6},{6,5},{7,4},{8,11},{9,10},{10,... | collective-permute-start | bytes 2312 | tf_op jit(solution)/shard_map/ppermute | solution.py:400
  21.7 0.0 copy-start.5
  21.7 0.0 copy-start.4
  21.7 0.0 copy-start.6
  21.7 0.0 collective-permute-start.5
  21.7 0.0 copy-done.1
  21.7 0.0 copy-done.3
  21.7 0.6 %copy-done.5 = f32[2,100]{1,0:T(2,128)S(1)} copy-done((f32[2,100]{1,0:T(2,128)S(1)}, f32[2,100]{1,0:T(2,128)}, u32[]{:S(2)}) %copy-start.5) | copy-done | bytes 824
  22.3 0.0 copy-done.4
  22.4 0.0 copy-done.6
  22.4 11.8 %atoms.1 = (f32[16,324]{1,0:T(8,128)}, f32[1,16]{1,0:T(1,128)}) custom-call(s32[1,1]{1,0:T(1,128)S(6)} %copy.20.count_ref, s32[1,1,16]{2,1,0:T(1,128)S(1)} %copy-done.6, f32[16,324]{1,0:T(8,128)S(1)} %bitcast.13, f32[2,18,5000]{2,1,0:T(8,128)S(1)} %copy.16.ae_ref, f32[2,18,5000]{2,1,0:T(8,128)S(1)} %copy.17.ps_ref, f32[2,100]{1,0:T(2,128)S(1)} %copy-done.4, ...), custom_call_target="tpu_custom_call" | custom-call | flops 207360000 | bytes 3145728 | tf_op jit(solution)/shard_map/atoms/pallas_call | solution.py:263
  34.2 0.0 copy-start
  34.2 0.0 collective-permute-done.4
  34.2 0.0 collective-permute-done.5
  34.2 0.1 maximum_bitcast_fusion
  34.3 0.0 copy-start.2
  34.4 0.8 %copy-done = bf16[528,288]{1,0:T(8,128)(2,1)S(1)} copy-done((bf16[528,288]{1,0:T(8,128)(2,1)S(1)}, bf16[528,288]{1,0:T(8,128)(2,1)}, u32[]{:S(2)}) %copy-start) | copy-done | bytes 304152
  35.2 0.1 copy-done.2
  35.2 1.7 %grid.1 = (f32[8,16,128]{2,1,0:T(8,128)}, f32[8,16,128]{2,1,0:T(8,128)}) custom-call(f32[96,68]{1,0:T(8,128)S(1)} %bitcast.12, bf16[528,288]{1,0:T(8,128)(2,1)S(1)} %copy-done, bf16[68,512]{1,0:T(8,128)(2,1)S(1)} %copy-done.2), custom_call_target="tpu_custom_call" | custom-call | flops 4915200 | bytes 2097152 | tf_op jit(solution)/shard_map/grid/pallas_call | solution.py:378
  (8 shorter events, 0.1 us)
Async XLA Ops:
  0.6 0.7 %copy-start.8 = (f32[4,8,64]{2,1,0:T(8,128)S(1)}, f32[4,8,64]{2,1,0:T(8,128)}, u32[]{:S(2)}) copy-start(f32[4,8,64]{2,1,0:T(8,128)} %param.11) | copy-start | bytes 24580
  1.4 9.8 %collective-permute-start = (f32[4,2,64]{2,1,0:T(2,128)S(1)}, f32[4,2,64]{2,1,0:T(2,128)S(1)}, u32[]{:S(2)}, u32[]{:S(2)}) collective-permute-start(f32[4,2,64]{2,1,0:T(2,128)S(1)} %get-tuple-element.20), channel_id=1, source_target_pairs={{0,12},{4,8},{8,4},{12,0},{1,13},{5,9},{9,5},{13,1},{2,14},{6,10},... | collective-permute-start | bytes 6152 | tf_op jit(solution)/shard_map/ppermute | solution.py:400
  9.7 1.5 %collective-permute-start.1 = (f32[4,2,64]{2,1,0:T(2,128)S(1)}, f32[4,2,64]{2,1,0:T(2,128)S(1)}, u32[]{:S(2)}, u32[]{:S(2)}) collective-permute-start(f32[4,2,64]{2,1,0:T(2,128)S(1)} %get-tuple-element.21), channel_id=1, source_target_pairs={{0,4},{4,0},{8,12},{12,8},{1,5},{5,1},{9,13},{13,9},{2,6},{6,2},{1... | collective-permute-start | bytes 6152 | tf_op jit(solution)/shard_map/ppermute | solution.py:399
  11.2 7.2 %collective-permute-start.2 = (f32[2,12,64]{2,1,0:T(8,128)S(1)}, f32[2,12,64]{2,1,0:T(8,128)S(1)}, u32[]{:S(2)}, u32[]{:S(2)}) collective-permute-start(f32[2,12,64]{2,1,0:T(8,128)S(1)} %get-tuple-element.18), channel_id=1, source_target_pairs={{0,240},{16,32},{32,16},{48,64},{64,48},{80,96},{96,80},{112,128},... | collective-permute-start | bytes 18440 | tf_op jit(solution)/shard_map/ppermute | solution.py:400
  16.0 2.6 %collective-permute-start.3 = (f32[2,12,64]{2,1,0:T(8,128)S(1)}, f32[2,12,64]{2,1,0:T(8,128)S(1)}, u32[]{:S(2)}, u32[]{:S(2)}) collective-permute-start(f32[2,12,64]{2,1,0:T(8,128)S(1)} %get-tuple-element.19), channel_id=1, source_target_pairs={{0,16},{16,0},{32,48},{48,32},{64,80},{80,64},{96,112},{112,96},{1... | collective-permute-start | bytes 18440 | tf_op jit(solution)/shard_map/ppermute | solution.py:399
  16.7 1.4 %copy-start.7 = (f32[2,18,5000]{2,0,1:T(2,128)S(1)}, f32[2,18,5000]{2,0,1:T(2,128)}, u32[]{:S(2)}) copy-start(f32[2,18,5000]{2,0,1:T(2,128)} %param.16) | copy-start | bytes 2160004
  18.6 3.1 %copy-start.1 = (f32[8,5120]{1,0:T(8,128)S(1)}, f32[8,5120]{1,0:T(8,128)}, u32[]{:S(2)}) copy-start(f32[8,5120]{1,0:T(8,128)} %constant.42.clone.radial_ref) | copy-start | bytes 491524
  18.6 3.1 %copy-start.3 = (f32[1,1,16,324]{3,2,1,0:T(8,128)S(1)}, f32[1,1,16,324]{3,2,1,0:T(8,128)}, u32[]{:S(2)}) copy-start(f32[1,1,16,324]{3,2,1,0:T(8,128)} %param.14) | copy-start | bytes 62212
  18.7 15.4 %collective-permute-start.4 = (f32[8,12,2]{2,1,0:T(8,128)S(1)}, f32[8,12,2]{2,1,0:T(8,128)S(1)}, u32[]{:S(2)}, u32[]{:S(2)}) collective-permute-start(f32[8,12,2]{2,1,0:T(8,128)S(1)} %get-tuple-element.14), channel_id=1, source_target_pairs={{0,3},{1,2},{2,1},{3,0},{4,7},{5,6},{6,5},{7,4},{8,11},{9,10},{10,... | collective-permute-start | bytes 2312 | tf_op jit(solution)/shard_map/ppermute | solution.py:400
  21.7 0.7 %copy-start.5 = (f32[2,100]{1,0:T(2,128)S(1)}, f32[2,100]{1,0:T(2,128)}, u32[]{:S(2)}) copy-start(f32[2,100]{1,0:T(2,128)} %ps_core_ref.1) | copy-start | bytes 2404
  21.7 0.7 %copy-start.4 = (f32[2,100]{1,0:T(2,128)S(1)}, f32[2,100]{1,0:T(2,128)}, u32[]{:S(2)}) copy-start(f32[2,100]{1,0:T(2,128)} %ae_core_ref.1) | copy-start | bytes 2404
  21.7 0.7 %copy-start.6 = (s32[1,1,16]{2,1,0:T(1,128)S(1)}, s32[1,1,16]{2,1,0:T(1,128)}, u32[]{:S(2)}) copy-start(s32[1,1,16]{2,1,0:T(1,128)} %species_ref.1) | copy-start | bytes 196
  21.7 12.5 %collective-permute-start.5 = (f32[8,12,2]{2,1,0:T(8,128)S(1)}, f32[8,12,2]{2,1,0:T(8,128)S(1)}, u32[]{:S(2)}, u32[]{:S(2)}) collective-permute-start(f32[8,12,2]{2,1,0:T(8,128)S(1)} %get-tuple-element.15), channel_id=1, source_target_pairs={{0,1},{1,0},{2,3},{3,2},{4,5},{5,4},{6,7},{7,6},{8,9},{9,8},{10,11... | collective-permute-start | bytes 2312 | tf_op jit(solution)/shard_map/ppermute | solution.py:399
  34.2 1.0 %copy-start = (bf16[528,288]{1,0:T(8,128)(2,1)S(1)}, bf16[528,288]{1,0:T(8,128)(2,1)}, u32[]{:S(2)}) copy-start(bf16[528,288]{1,0:T(8,128)(2,1)} %constant.40.clone.left_ref) | copy-start | bytes 912388
  34.3 0.9 %copy-start.2 = (bf16[68,512]{1,0:T(8,128)(2,1)S(1)}, bf16[68,512]{1,0:T(8,128)(2,1)}, u32[]{:S(2)}) copy-start(bf16[68,512]{1,0:T(8,128)(2,1)} %constant.41.clone.right_ref) | copy-start | bytes 208900

commit v2 on v1

v2 whole, which is shorter than its diff:
```python
import functools
import math

import jax
import jax.numpy as jnp
import numpy as np
from jax import lax
from jax.experimental import pallas as pl
from jax.experimental.pallas import tpu as pltpu
from jax.sharding import PartitionSpec as P

fine_step = 0.1
sphere_radius = 2.5
enhance_kappa = 0.804
enhance_mu = 0.2195149727645171
gradient_beta = 0.06672455060314922
gradient_gamma = (1.0 - math.log(2.0)) / math.pi**2
perdew_amplitude = 0.031091
perdew_alpha = 0.2137
perdew_first = 7.5957
perdew_second = 3.5876
perdew_third = 1.6382
perdew_fourth = 0.49294

exchange_scale = -0.75 * (3.0 / math.pi) ** (1.0 / 3.0)
fermi_scale = (3.0 * math.pi**2) ** (1.0 / 3.0)
radius_scale = (3.0 / (4.0 * math.pi)) ** (1.0 / 3.0)
reduced_scale = 1.0 / (4.0 * fermi_scale**2)
scaled_scale = math.pi / (16.0 * fermi_scale)
beta_ratio = gradient_beta / gradient_gamma
fit = [
    2.0 * perdew_amplitude * c * radius_scale ** (k / 2.0)
    for k, c in ((1, perdew_first), (2, perdew_second), (3, perdew_third), (4, perdew_fourth))
]
ln2 = math.log(2.0)
third = perdew_amplitude / 3.0


def functional(n, s):
    m = jnp.exp2(jnp.log2(n) * (-1.0 / 6.0))
    m2 = m * m
    m4 = m2 * m2
    m8 = m4 * m4
    by_p = (enhance_mu / enhance_kappa * reduced_scale) * (m8 * m8)
    by_t = (beta_ratio * scaled_scale) * (m8 * m4 * m2)
    fitted = m * (fit[0] + m * (fit[1] + m * (fit[2] + m * fit[3])))
    slope = m * (
        third * fit[0]
        + m * (2.0 * third * fit[1] + m * (3.0 * third * fit[2] + m * (4.0 * third * fit[3])))
    )
    one_fit = 1.0 + fitted
    enhance = 1.0 + s * by_p
    fit_both = fitted * one_fit
    joint = 1.0 / (fit_both * enhance)
    inverse_fit = joint * enhance
    damp = joint * fit_both
    log_term = jnp.log2(1.0 + one_fit * inverse_fit)
    alpha_r = (perdew_alpha * radius_scale) * m2
    one_alpha = 1.0 + alpha_r
    product_c = one_alpha * log_term
    inv_exp = 1.0 / (jnp.exp2((2.0 * perdew_amplitude / gradient_gamma) * product_c) - 1.0)
    c_n = (2.0 * ln2 * third) * (alpha_r * log_term) - one_alpha * (slope * inverse_fit)
    t = s * by_t
    q = t * inv_exp
    num = 1.0 + q
    den_inv = 1.0 / (1.0 + q * num)
    z = 1.0 + t * (num * den_inv)
    z_inv = 1.0 / z
    den_z = den_inv * z_inv
    h_t = ((num + q) * den_inv) * den_z
    h_c = (t * (q * den_inv)) * ((q * (1.0 + num)) * den_z) * (1.0 + inv_exp)
    ch = (gradient_gamma * ln2) * jnp.log2(z) - (2.0 * perdew_amplitude * ln2) * product_c
    x = (enhance_kappa * exchange_scale) * (n * m4)
    xf = x * ((1.0 + 1.0 / enhance_kappa) - damp)
    xd = x * damp
    e = n * (xf + ch)
    e_n = (
        (4.0 / 3.0) * xf
        + (8.0 / 3.0) * (xd * (damp - 1.0))
        + ch
        + (c_n - h_c * c_n)
        - (7.0 / 3.0 * gradient_gamma) * (h_t * t)
    )
    e_s = n * ((xd * damp) * by_p + gradient_gamma * (h_t * by_t))
    return e, e_n, e_s


ROW = 24


def radial_table(nrad, npts, width):
    g = np.arange(width) % nrad
    live = np.arange(width) < npts
    r = sphere_radius * (g + 0.5) / nrad
    w = r * r * (sphere_radius / nrad)
    k = nrad / sphere_radius
    up = np.where(g == nrad - 1, 0.0, np.where(g == 0, k, 0.5 * k))
    down = np.where(g == 0, 0.0, np.where(g == nrad - 1, -k, -0.5 * k))
    mid = np.where(g == 0, -k, np.where(g == nrad - 1, k, 0.0))
    rows = np.stack([w, up, mid, down] + [np.zeros(width)] * 4) * live
    return rows.astype(np.float32)


def atoms_kernel(
    ni, nrad, npts, na, units,
    count_ref, species_ref, d_ref, ae_ref, ps_ref, ae_core_ref, ps_core_ref, radial_ref,
    h_in_ref, e_in_ref, h_ref, e_ref,
    lhs32, cores, total, *scratch,
):
    f32, bf16 = jnp.float32, jnp.bfloat16
    row = lax.broadcasted_iota(jnp.int32, (na, 128), 0)
    species = jnp.zeros((na, 128), jnp.int32)
    for a in range(na):
        species = jnp.where(row == a, species_ref[0, 0, a], species)
    first = species == 0
    first_f = jnp.where(first, 1.0, 0.0).astype(f32)
    second_f = 1.0 - first_f

    lhs32[...] = jnp.zeros_like(lhs32)
    for i in range(ni):
        d = d_ref[:, ni * i : ni * (i + 1)]
        d1 = d.astype(bf16).astype(f32)
        d2 = d - d1
        here = pl.ds(na * i, na)
        for block, part in ((0, d1), (1, d1), (2, d2)):
            at = 2 * ROW * block
            lhs32[here, at : at + ni] = part * first_f[:, :ni]
            lhs32[here, at + ROW : at + ROW + ni] = part * second_f[:, :ni]
    lhs = lhs32[:, 0 : 6 * ROW].astype(bf16)

    longest = max(high - low for _, low, high in units)
    cores[0:2, 0:nrad] = ae_core_ref[...]
    cores[2:4, 0:nrad] = ps_core_ref[...]
    reach = nrad
    while reach < longest:
        more = min(reach, longest - reach)
        cores[0:4, reach : reach + more] = cores[0:4, 0:more]
        reach += more

    e_sum = jnp.zeros((na, 128), f32)
    for u, (table, low, high) in enumerate(units):
        waves, packed, rho, part_q = scratch[4 * u : 4 * u + 4]
        x_ref = (ae_ref, ps_ref)[table]
        size, live = high - low, min(high, npts) - low
        tail = live // 128 * 128
        if tail < size:
            waves[:, tail:] = jnp.zeros((2 * ROW, size - tail), f32)
        for s in range(2):
            waves[ROW * s + 16 : ROW * (s + 1), 0:tail] = jnp.zeros((ROW - 16, tail), f32)
            waves[ROW * s : ROW * s + ni, 0:live] = x_ref[s, :, low : low + live]
        pick = jnp.concatenate([first] * (size // 128), axis=1)

        x = waves[...]
        x1 = x.astype(bf16)
        x2 = (x - x1.astype(f32)).astype(bf16)
        packed[...] = jnp.concatenate([x1, x2], axis=0)
        mixed = jnp.dot(lhs, jnp.concatenate([x1, x2, x1], axis=0), preferred_element_type=f32)
        n = jnp.where(
            pick,
            cores[2 * table : 2 * table + 1, 0:size],
            cores[2 * table + 1 : 2 * table + 2, 0:size],
        )
        for i in range(ni):
            own = jnp.where(pick, x[i : i + 1], x[ROW + i : ROW + i + 1])
            n = n + own * mixed[na * i : na * (i + 1)]
        rho[...] = n

        scale = (-1.0 if table else 1.0) * 4.0 * math.pi * nrad / npts
        n = rho[...]
        radial = radial_ref[:, low:high]
        weight = radial[0:1] * scale
        up, mid, down = radial[1:2], radial[2:3], radial[3:4]
        slope = up * pltpu.roll(n, size - 1, 1) + mid * n + down * pltpu.roll(n, 1, 1)
        e, e_n, e_s = functional(n, slope * slope)
        we = e * weight
        for j in range(size // 128):
            e_sum = e_sum + we[:, 128 * j : 128 * (j + 1)]
        part_q[...] = (slope * e_s) * (2.0 * weight)
        q = part_q[...]
        g = e_n * weight + mid * q
        g = g + radial[5:6] * pltpu.roll(q, 1, 1) + radial[6:7] * pltpu.roll(q, size - 1, 1)
        rho[...] = g
        g = rho[...]
        x = waves[...]
        hi, lo = [], []
        for i in range(ni):
            own = jnp.where(pick, x[i : i + 1], x[ROW + i : ROW + i + 1]) * g
            top = own.astype(bf16)
            hi.append(top)
            lo.append((own - top.astype(f32)).astype(bf16))
        out = lax.dot_general(
            jnp.concatenate(hi + lo, axis=0), packed[...], (((1,), (1,)), ((), ())),
            preferred_element_type=f32,
        )
        if u == 0:
            total[...] = out
        else:
            total[...] += out

    tally = count_ref[0, 0]
    live = row < tally
    for i in range(ni):
        both = total[na * i : na * (i + 1), :] + total[na * (ni + i) : na * (ni + i + 1), :]
        value = both[:, 0 : 2 * ROW] + both[:, 2 * ROW : 4 * ROW]
        value = jnp.where(first[:, :ni], value[:, 0:ni], value[:, ROW : ROW + ni])
        here = slice(ni * i, ni * (i + 1))
        h_ref[:, here] = h_in_ref[:, here] + jnp.where(live[:, :ni], value, 0.0)
    energy = jnp.sum(e_sum, axis=1, keepdims=True)
    energy = jnp.where(live[:, :1], energy, 0.0)
    diagonal = lax.broadcasted_iota(jnp.int32, (na, na), 0) == lax.broadcasted_iota(
        jnp.int32, (na, na), 1
    )
    e_ref[...] = e_in_ref[...] + jnp.sum(jnp.where(diagonal, energy, 0.0), axis=0, keepdims=True)


def atom_terms(units, sums, count, species, matrices, ae, ps, ae_core, ps_core):
    na, pairs = matrices.shape
    ni, npts = ae.shape[1], ae.shape[2]
    nrad = ae_core.shape[1]
    width = -(-npts // 128) * 128
    radial = radial_table(nrad, npts, width)
    radial[5] = np.roll(radial[1], 1)
    radial[6] = np.roll(radial[3], -1)
    vmem = pl.BlockSpec(memory_space=pltpu.VMEM)
    smem = pl.BlockSpec(memory_space=pltpu.SMEM)
    f32, bf16 = jnp.float32, jnp.bfloat16
    points = sum(high - low for _, low, high in units)
    scratch = [
        pltpu.VMEM((na * ni, 256), f32),
        pltpu.VMEM((8, max(high - low for _, low, high in units)), f32),
        pltpu.VMEM((2 * na * ni, 4 * ROW), f32),
    ]
    for _, low, high in units:
        scratch += [
            pltpu.VMEM((2 * ROW, high - low), f32),
            pltpu.VMEM((4 * ROW, high - low), bf16),
            pltpu.VMEM((na, high - low), f32),
            pltpu.VMEM((na, high - low), f32),
        ]
    return pl.pallas_call(
        functools.partial(atoms_kernel, ni, nrad, npts, na, units),
        out_shape=(
            jax.ShapeDtypeStruct((na, pairs), f32),
            jax.ShapeDtypeStruct((1, na), f32),
        ),
        in_specs=[smem, smem] + [vmem] * 8,
        out_specs=(vmem, vmem),
        scratch_shapes=scratch,
        compiler_params=pltpu.CompilerParams(vmem_limit_bytes=40 << 20),
        cost_estimate=pl.CostEstimate(
            flops=4 * na * ni * ni * points, transcendentals=na * points * 10, bytes_accessed=2 << 20
        ),
        name="atoms",
    )(count, species, matrices, ae, ps, ae_core, ps_core, jnp.asarray(radial), *sums)


def upsampling(cells, halo):
    table = np.zeros((2 * cells + 4, cells + 2 * halo))
    for k in range(-2, 2 * cells + 2):
        i = k // 2
        table[k + 2, i + halo] = 0.75
        table[k + 2, i + halo + (1 if k % 2 else -1)] = 0.25
    return table


def grid_tables(nx, ny, nz):
    ux, uy, uz = upsampling(nx, 2), upsampling(ny, 2), upsampling(nz, 2)
    fx, fy, fz = 2 * nx, 2 * ny, 2 * nz

    def diff(u):
        return np.concatenate([np.zeros_like(u[:1]), u[2:] - u[:-2], np.zeros_like(u[:1])])

    places = [(-1, y) for y in range(fy)]
    places += [(x, y) for x in range(fx) for y in range(fy)]
    places += [(fx, y) for y in range(fy)]
    places += [(x, -1) for x in range(fx)] + [(x, fy) for x in range(fx)]

    def rows(wx, wy):
        return np.stack([np.outer(wy[y + 2], wx[x + 2]).reshape(-1) for x, y in places])

    left = np.concatenate([rows(ux, uy), rows(diff(ux), uy), rows(ux, diff(uy))])
    beyond = np.array([fz] + [fz // 2] * (fz - 2) + [-1])
    right = np.concatenate(
        [w[at + 2] for w in (uz, diff(uz)) for at in (np.arange(fz), beyond)]
    ).T
    return np.concatenate([left] * 3, axis=1), right


def split3(x):
    f32, bf16 = jnp.float32, jnp.bfloat16
    x1 = x.astype(bf16)
    rest = x - x1.astype(f32)
    x2 = rest.astype(bf16)
    return x1, x2, (rest - x2.astype(f32)).astype(bf16)


def grid_kernel(fx, fy, fz, c_ref, left_ref, right_ref, v_ref, e_ref):
    f32 = jnp.float32
    right = right_ref[...]
    parts = [jnp.dot(p, right, preferred_element_type=f32) for p in split3(c_ref[...])]
    lines = parts[0] + (parts[1] + parts[2])
    stack = jnp.concatenate(split3(lines), axis=0)
    inner = fx * fy
    rows = inner + 2 * fy + 2 * fx
    plane = jnp.dot(left_ref[...], stack[:, : 2 * fz], preferred_element_type=f32)
    dz_all = jnp.dot(left_ref[0:rows, :], stack[:, 2 * fz :], preferred_element_type=f32)
    inv = 0.5 / fine_step

    def fields(lo, hi, tile):
        cols = slice(fz * tile, fz * (tile + 1))
        n, dx, dy = (plane[rows * k + lo : rows * k + hi, cols] for k in range(3))
        dz = dz_all[lo:hi, cols]
        s = (inv * inv) * (dx * dx + dy * dy + dz * dz)
        return functional(n, s), dx, dy, dz

    main = slice(fy, fy + inner)
    (e, e_n, e_s), dx, dy, dz = fields(fy, fy + inner, 0)
    e_ref[...] = e.reshape(fx, fy, fz)
    (_, _, s_low), dx_low, _, _ = fields(0, fy, 0)
    (_, _, s_high), dx_high, _, _ = fields(fy + inner, 2 * fy + inner, 0)
    (_, _, s_side), _, dy_side, _ = fields(2 * fy + inner, rows, 0)
    (_, _, s_end), _, _, dz_end = fields(fy, fy + inner, 1)
    flux_x = jnp.concatenate([s_low * dx_low, e_s * dx, s_high * dx_high], axis=0)
    change = flux_x[2 * fy :] - flux_x[: inner]
    flux_z, end_z = e_s * dz, s_end * dz_end
    lane = lax.broadcasted_iota(jnp.int32, (inner, fz), 1)
    after = pltpu.roll(jnp.where(lane == 0, end_z, flux_z), fz - 1, 1)
    before = pltpu.roll(jnp.where(lane == fz - 1, end_z, flux_z), 1, 1)
    change = change + (after - before)
    flux_y, side_y = e_s * dy, s_side * dy_side
    line = lax.broadcasted_iota(jnp.int32, (fy, fz), 0)
    for x in range(fx):
        here = slice(fy * x, fy * (x + 1))
        own = flux_y[here]
        after = jnp.where(line == fy - 1, side_y[fx + x : fx + x + 1], pltpu.roll(own, fy - 1, 0))
        before = jnp.where(line == 0, side_y[x : x + 1], pltpu.roll(own, 1, 0))
        v_ref[x] = e_n[here] - (2.0 * inv * inv) * (change[here] + (after - before))


def grid_terms(columns, nx, ny, nz):
    left, right = grid_tables(nx, ny, nz)
    fx, fy, fz = 2 * nx, 2 * ny, 2 * nz
    vmem = pl.BlockSpec(memory_space=pltpu.VMEM)
    fine = jax.ShapeDtypeStruct((fx, fy, fz), jnp.float32)
    return pl.pallas_call(
        functools.partial(grid_kernel, fx, fy, fz),
        out_shape=(fine, fine),
        in_specs=[vmem] * 3,
        out_specs=(vmem, vmem),
        compiler_params=pltpu.CompilerParams(vmem_limit_bytes=32 << 20),
        cost_estimate=pl.CostEstimate(
            flops=300 * fx * fy * fz, transcendentals=10 * fx * fy * fz, bytes_accessed=2 << 20
        ),
        name="grid",
    )(columns, jnp.asarray(left, jnp.bfloat16), jnp.asarray(right, jnp.bfloat16))


def with_halo(cells, axis, dim, width, work, sums):
    count = lax.axis_size(axis)
    even = lax.axis_index(axis) % 2 == 0
    head = lax.slice_in_dim(cells, 0, width, axis=dim)
    tail = lax.slice_in_dim(cells, cells.shape[dim] - width, cells.shape[dim], axis=dim)
    inner = [(i, i ^ 1) for i in range(count)]
    outer = [(i, (i + 1 if i % 2 else i - 1) % count) for i in range(count)]
    first = lax.ppermute(jnp.where(even, tail, head), axis, inner)
    second = lax.ppermute(jnp.where(even, head, tail), axis, outer)
    sums = work(sums)
    first, second, sums = lax.optimization_barrier((first, second, sums))
    return (
        jnp.concatenate(
            [jnp.where(even, second, first), cells, jnp.where(even, first, second)], axis=dim
        ),
        sums,
    )


def shards(
    coarse_density,
    atom_count,
    atom_species,
    density_matrix,
    partial_waves,
    smooth_waves,
    core_density,
    smooth_core,
):
    slots, pairs = density_matrix.shape[2:]
    owned = (
        atom_count,
        atom_species,
        density_matrix.reshape(slots, pairs),
        partial_waves,
        smooth_waves,
        core_density,
        smooth_core,
    )
    sums = (jnp.zeros((slots, pairs), jnp.float32), jnp.zeros((1, slots), jnp.float32))
    cells = coarse_density
    runs = [(), ((0, 0, 3200), (0, 3200, 5120)), ((1, 0, 3200), (1, 3200, 5120))]
    for (axis, dim), units in zip((("gy", 1), ("gx", 0), ("gz", 2)), runs):
        cells, sums = with_halo(
            cells, axis, dim, 2, lambda s: atom_terms(units, s, *owned) if units else s, sums
        )
    placed, placed_energy = sums
    columns = cells.transpose(1, 0, 2).reshape(-1, cells.shape[2])
    potential, energy_density = grid_terms(columns, *coarse_density.shape)
    return (
        potential,
        energy_density,
        placed.reshape(density_matrix.shape),
        placed_energy.reshape(atom_species.shape),
    )


def solution(mesh):
    in_specs = (
        P("gx", "gy", "gz"),
        P("gx", ("gy", "gz")),
        P("gx", ("gy", "gz"), None),
        P("gx", ("gy", "gz"), None, None),
        P(),
        P(),
        P(),
        P(),
    )
    out_specs = (
        P("gx", "gy", "gz"),
        P("gx", "gy", "gz"),
        P("gx", ("gy", "gz"), None, None),
        P("gx", ("gy", "gz"), None),
    )
    return jax.shard_map(shards, mesh=mesh, in_specs=in_specs, out_specs=out_specs, check_vma=False)
```

time: 37.2 us -> 34.2 us (0.919)
  waiting for transfers between devices: 1.71 us -> 0.02 us
  starting transfers between devices: 16 us -> 15.1 us
  Pallas kernels: 13.5 us -> 13 us
    ppermute x3, waiting for transfers between devices: 1.49 us -> 0.01 us  [with_halo(): second = lax.ppermute(jnp.where(even, head, tail), axis, outer)]
    ppermute x3, starting transfers between devices: 16 us -> 15.1 us  [with_halo(): second = lax.ppermute(jnp.where(even, head, tail), axis, outer)]
    pallas_call x1 -> x2, Pallas kernels: 11.8 us -> 11.3 us  [atom_terms(): pl.pallas_call(functools.partial(atoms_kernel, ni, nrad, npts, na, units)...]
  transfers between devices with their start and end apart: 6 -> 6, of which waited for: 2 -> 0; matrix products, arithmetic and copies ran while one was open for 5% -> 5% of each run, Pallas kernels for 32% -> 33%
where the time goes in v2:
time: 34.2 us; the launch traced here: 33.9 us
  starting transfers between devices  15.1 us (44%)
  Pallas kernels  13 us (38%)
  local copies, waits for them, and re-layouts  3.95 us (12%)
  between operations  1.51 us (4%)
    ppermute x3, starting transfers between devices, with_halo(): second = lax.ppermute(jnp.where(even, head, tail), axis, outer)  15.1 us
    pallas_call x2, Pallas kernels, atom_terms(): pl.pallas_call(functools.partial(atoms_kernel, ni, nrad, npts, na, units)...  11.3 us
    unnamed x20, local copies, waits for them, and re-layouts  3.93 us
    pallas_call x1, Pallas kernels, grid_terms(): pl.pallas_call(functools.partial(grid_kernel, fx, fy, fz), out_shape=(fin...  1.67 us
  transfers between devices with their start and end apart: 6, of which 0 were waited for; matrix products, arithmetic and copies ran while one was open for 5% of the time, Pallas kernels for 33%

profile of v2, /device:TPU:1, one launch (start us, length us, event | category | flops | bytes accessed | tf_op | source)
XLA Modules:
  0.0 33.9 jit_solution(16720029307585972859)
XLA Ops:
  0.6 0.0 copy-start.8
  0.7 0.7 %copy-done.8 = f32[4,8,64]{2,1,0:T(8,128)S(1)} copy-done((f32[4,8,64]{2,1,0:T(8,128)S(1)}, f32[4,8,64]{2,1,0:T(8,128)}, u32[]{:S(2)}) %copy-start.8) | copy-done | bytes 8216
  1.4 8.3 %collective-permute-start.1 = (f32[4,2,64]{2,1,0:T(2,128)S(1)}, f32[4,2,64]{2,1,0:T(2,128)S(1)}, u32[]{:S(2)}, u32[]{:S(2)}) collective-permute-start(f32[4,2,64]{2,1,0:T(2,128)S(1)} %get-tuple-element.48), channel_id=1, source_target_pairs={{0,12},{4,8},{8,4},{12,0},{1,13},{5,9},{9,5},{13,1},{2,14},{6,10},... | collective-permute-start | bytes 6152 | tf_op jit(solution)/shard_map/ppermute | solution.py:366
  9.7 0.0 collective-permute-start
  10.3 0.0 copy-start.7
  10.3 1.4 %copy.16.ae_ref = f32[2,18,5000]{2,1,0:T(8,128)S(1)} copy(f32[2,18,5000]{2,0,1:T(2,128)} %param.16) | data formatting | bytes 1440000 | tf_op args[4]
  11.8 0.0 copy-done.7
  11.8 0.0 copy-start.2
  11.8 0.2 copy.17.ps_ref
  12.0 0.0 copy-start
  12.0 0.0 collective-permute-done.1
  12.1 0.0 collective-permute-done
  12.1 5.0 %collective-permute-start.3 = (f32[2,12,64]{2,1,0:T(8,128)S(1)}, f32[2,12,64]{2,1,0:T(8,128)S(1)}, u32[]{:S(2)}, u32[]{:S(2)}) collective-permute-start(f32[2,12,64]{2,1,0:T(8,128)S(1)} %get-tuple-element.46), channel_id=1, source_target_pairs={{0,240},{16,32},{32,16},{48,64},{64,48},{80,96},{96,80},{112,128},... | collective-permute-start | bytes 18440 | tf_op jit(solution)/shard_map/ppermute | solution.py:366
  17.1 0.0 collective-permute-start.2
  17.1 0.0 copy-start.4
  17.1 0.0 copy-start.5
  17.1 0.0 copy-start.6
  17.2 0.0 copy-done.2
  17.2 0.0 copy-done
  17.2 0.6 %copy-done.4 = f32[2,100]{1,0:T(2,128)S(1)} copy-done((f32[2,100]{1,0:T(2,128)S(1)}, f32[2,100]{1,0:T(2,128)}, u32[]{:S(2)}) %copy-start.4) | copy-done | bytes 824
  17.8 0.0 copy-done.5
  17.8 0.0 copy-done.6
  17.8 5.4 %atoms.2 = (f32[16,324]{1,0:T(8,128)S(1)}, f32[1,16]{1,0:T(1,128)S(1)}) custom-call(s32[1,1]{1,0:T(1,128)S(6)} %copy.23.count_ref, s32[1,1,16]{2,1,0:T(1,128)S(1)} %copy-done.6, f32[16,324]{1,0:T(8,128)S(1)} %bitcast.13, f32[2,18,5000]{2,1,0:T(8,128)S(1)} %copy.16.ae_ref, f32[2,18,5000]{2,1,0:T(8,128)S(1)} %copy.17.ps_ref, f32[2,100]{1,0:T(2,128)S(1)} %copy-done.4, ...), custom_call_target="tpu_custom_call" | custom-call | flops 106168320 | bytes 2097152 | tf_op jit(solution)/shard_map/atoms/pallas_call | solution.py:240
  23.2 0.0 collective-permute-done.3
  23.2 0.0 collective-permute-done.2
  23.3 0.1 slice_select_fusion
  23.3 1.8 %collective-permute-start.5 = (f32[8,12,2]{2,1,0:T(8,128)S(1)}, f32[8,12,2]{2,1,0:T(8,128)S(1)}, u32[]{:S(2)}, u32[]{:S(2)}) collective-permute-start(f32[8,12,2]{2,1,0:T(8,128)S(1)} %get-tuple-element.42), channel_id=1, source_target_pairs={{0,3},{1,2},{2,1},{3,0},{4,7},{5,6},{6,5},{7,4},{8,11},{9,10},{10,... | collective-permute-start | bytes 2312 | tf_op jit(solution)/shard_map/ppermute | solution.py:366
  25.1 0.0 collective-permute-start.4
  25.1 6.0 %atoms.3 = (f32[16,324]{1,0:T(8,128)}, f32[1,16]{1,0:T(1,128)}) custom-call(s32[1,1]{1,0:T(1,128)S(6)} %copy.23.count_ref, s32[1,1,16]{2,1,0:T(1,128)S(1)} %copy-done.6, f32[16,324]{1,0:T(8,128)S(1)} %bitcast.14, f32[2,18,5000]{2,1,0:T(8,128)S(1)} %copy.16.ae_ref, f32[2,18,5000]{2,1,0:T(8,128)S(1)} %copy.17.ps_ref, f32[2,100]{1,0:T(2,128)S(1)} %copy-done.4, ...), custom_call_target="tpu_custom_call" | custom-call | flops 106168320 | bytes 2097152 | tf_op jit(solution)/shard_map/atoms/pallas_call | solution.py:240
  31.1 0.0 copy-start.1
  31.1 0.0 collective-permute-done.5
  31.1 0.0 collective-permute-done.4
  31.2 0.1 maximum_bitcast_fusion
  31.3 0.0 copy-start.3
  31.3 0.8 %copy-done.1 = bf16[528,288]{1,0:T(8,128)(2,1)S(1)} copy-done((bf16[528,288]{1,0:T(8,128)(2,1)S(1)}, bf16[528,288]{1,0:T(8,128)(2,1)}, u32[]{:S(2)}) %copy-start.1) | copy-done | bytes 304152
  32.1 0.1 copy-done.3
  32.2 1.7 %grid.1 = (f32[8,16,128]{2,1,0:T(8,128)}, f32[8,16,128]{2,1,0:T(8,128)}) custom-call(f32[96,68]{1,0:T(8,128)S(1)} %bitcast.12, bf16[528,288]{1,0:T(8,128)(2,1)S(1)} %copy-done.1, bf16[68,512]{1,0:T(8,128)(2,1)S(1)} %copy-done.3), custom_call_target="tpu_custom_call" | custom-call | flops 4915200 | bytes 2097152 | tf_op jit(solution)/shard_map/grid/pallas_call | solution.py:345
  (10 shorter events, 0.1 us)
Async XLA Ops:
  0.6 0.7 %copy-start.8 = (f32[4,8,64]{2,1,0:T(8,128)S(1)}, f32[4,8,64]{2,1,0:T(8,128)}, u32[]{:S(2)}) copy-start(f32[4,8,64]{2,1,0:T(8,128)} %param.12) | copy-start | bytes 24580
  1.4 10.7 %collective-permute-start.1 = (f32[4,2,64]{2,1,0:T(2,128)S(1)}, f32[4,2,64]{2,1,0:T(2,128)S(1)}, u32[]{:S(2)}, u32[]{:S(2)}) collective-permute-start(f32[4,2,64]{2,1,0:T(2,128)S(1)} %get-tuple-element.48), channel_id=1, source_target_pairs={{0,12},{4,8},{8,4},{12,0},{1,13},{5,9},{9,5},{13,1},{2,14},{6,10},... | collective-permute-start | bytes 6152 | tf_op jit(solution)/shard_map/ppermute | solution.py:366
  9.7 2.4 %collective-permute-start = (f32[4,2,64]{2,1,0:T(2,128)S(1)}, f32[4,2,64]{2,1,0:T(2,128)S(1)}, u32[]{:S(2)}, u32[]{:S(2)}) collective-permute-start(f32[4,2,64]{2,1,0:T(2,128)S(1)} %get-tuple-element.49), channel_id=1, source_target_pairs={{0,4},{4,0},{8,12},{12,8},{1,5},{5,1},{9,13},{13,9},{2,6},{6,2},{1... | collective-permute-start | bytes 6152 | tf_op jit(solution)/shard_map/ppermute | solution.py:365
  10.3 1.4 %copy-start.7 = (f32[2,18,5000]{2,0,1:T(2,128)S(1)}, f32[2,18,5000]{2,0,1:T(2,128)}, u32[]{:S(2)}) copy-start(f32[2,18,5000]{2,0,1:T(2,128)} %param.17) | copy-start | bytes 2160004
  11.8 5.4 %copy-start.2 = (f32[1,1,16,324]{3,2,1,0:T(8,128)S(1)}, f32[1,1,16,324]{3,2,1,0:T(8,128)}, u32[]{:S(2)}) copy-start(f32[1,1,16,324]{3,2,1,0:T(8,128)} %param.15) | copy-start | bytes 62212
  12.0 5.1 %copy-start = (f32[8,5120]{1,0:T(8,128)S(1)}, f32[8,5120]{1,0:T(8,128)}, u32[]{:S(2)}) copy-start(f32[8,5120]{1,0:T(8,128)} %constant.43.clone.radial_ref) | copy-start | bytes 491524
  12.1 11.1 %collective-permute-start.3 = (f32[2,12,64]{2,1,0:T(8,128)S(1)}, f32[2,12,64]{2,1,0:T(8,128)S(1)}, u32[]{:S(2)}, u32[]{:S(2)}) collective-permute-start(f32[2,12,64]{2,1,0:T(8,128)S(1)} %get-tuple-element.46), channel_id=1, source_target_pairs={{0,240},{16,32},{32,16},{48,64},{64,48},{80,96},{96,80},{112,128},... | collective-permute-start | bytes 18440 | tf_op jit(solution)/shard_map/ppermute | solution.py:366
  17.1 6.1 %collective-permute-start.2 = (f32[2,12,64]{2,1,0:T(8,128)S(1)}, f32[2,12,64]{2,1,0:T(8,128)S(1)}, u32[]{:S(2)}, u32[]{:S(2)}) collective-permute-start(f32[2,12,64]{2,1,0:T(8,128)S(1)} %get-tuple-element.47), channel_id=1, source_target_pairs={{0,16},{16,0},{32,48},{48,32},{64,80},{80,64},{96,112},{112,96},{1... | collective-permute-start | bytes 18440 | tf_op jit(solution)/shard_map/ppermute | solution.py:365
  17.1 0.7 %copy-start.4 = (f32[2,100]{1,0:T(2,128)S(1)}, f32[2,100]{1,0:T(2,128)}, u32[]{:S(2)}) copy-start(f32[2,100]{1,0:T(2,128)} %ae_core_ref.3) | copy-start | bytes 2404
  17.1 0.7 %copy-start.5 = (f32[2,100]{1,0:T(2,128)S(1)}, f32[2,100]{1,0:T(2,128)}, u32[]{:S(2)}) copy-start(f32[2,100]{1,0:T(2,128)} %ps_core_ref.3) | copy-start | bytes 2404
  17.1 0.7 %copy-start.6 = (s32[1,1,16]{2,1,0:T(1,128)S(1)}, s32[1,1,16]{2,1,0:T(1,128)}, u32[]{:S(2)}) copy-start(s32[1,1,16]{2,1,0:T(1,128)} %species_ref.3) | copy-start | bytes 196
  23.3 7.8 %collective-permute-start.5 = (f32[8,12,2]{2,1,0:T(8,128)S(1)}, f32[8,12,2]{2,1,0:T(8,128)S(1)}, u32[]{:S(2)}, u32[]{:S(2)}) collective-permute-start(f32[8,12,2]{2,1,0:T(8,128)S(1)} %get-tuple-element.42), channel_id=1, source_target_pairs={{0,3},{1,2},{2,1},{3,0},{4,7},{5,6},{6,5},{7,4},{8,11},{9,10},{10,... | collective-permute-start | bytes 2312 | tf_op jit(solution)/shard_map/ppermute | solution.py:366
  25.1 6.0 %collective-permute-start.4 = (f32[8,12,2]{2,1,0:T(8,128)S(1)}, f32[8,12,2]{2,1,0:T(8,128)S(1)}, u32[]{:S(2)}, u32[]{:S(2)}) collective-permute-start(f32[8,12,2]{2,1,0:T(8,128)S(1)} %get-tuple-element.43), channel_id=1, source_target_pairs={{0,1},{1,0},{2,3},{3,2},{4,5},{5,4},{6,7},{7,6},{8,9},{9,8},{10,11... | collective-permute-start | bytes 2312 | tf_op jit(solution)/shard_map/ppermute | solution.py:365
  31.1 1.0 %copy-start.1 = (bf16[528,288]{1,0:T(8,128)(2,1)S(1)}, bf16[528,288]{1,0:T(8,128)(2,1)}, u32[]{:S(2)}) copy-start(bf16[528,288]{1,0:T(8,128)(2,1)} %constant.44.clone.left_ref) | copy-start | bytes 912388
  31.3 0.9 %copy-start.3 = (bf16[68,512]{1,0:T(8,128)(2,1)S(1)}, bf16[68,512]{1,0:T(8,128)(2,1)}, u32[]{:S(2)}) copy-start(bf16[68,512]{1,0:T(8,128)(2,1)} %constant.45.clone.right_ref) | copy-start | bytes 208900

commit v3 on v2

--- a/solution.py
+++ b/solution.py
@@ -88,34 +88,35 @@
 ROW = 24
 
 
-def radial_table(nrad, npts, width):
-    g = np.arange(width) % nrad
-    live = np.arange(width) < npts
+RADIAL = 8
+
+
+def radial_table(nrad):
+    g = np.arange(nrad)
     r = sphere_radius * (g + 0.5) / nrad
-    w = r * r * (sphere_radius / nrad)
     k = nrad / sphere_radius
     up = np.where(g == nrad - 1, 0.0, np.where(g == 0, k, 0.5 * k))
     down = np.where(g == 0, 0.0, np.where(g == nrad - 1, -k, -0.5 * k))
     mid = np.where(g == 0, -k, np.where(g == nrad - 1, k, 0.0))
-    rows = np.stack([w, up, mid, down] + [np.zeros(width)] * 4) * live
-    return rows.astype(np.float32)
-
-
-def atoms_kernel(
-    ni, nrad, npts, na, units,
-    count_ref, species_ref, d_ref, ae_ref, ps_ref, ae_core_ref, ps_core_ref, radial_ref,
-    h_in_ref, e_in_ref, h_ref, e_ref,
-    lhs32, cores, total, *scratch,
-):
-    f32, bf16 = jnp.float32, jnp.bfloat16
+    rows = [r * r * (sphere_radius / nrad), up, mid, down, np.roll(up, 1), np.roll(down, -1)]
+    return np.stack(rows + [np.zeros(nrad)] * 2).astype(np.float32)
+
+
+def first_species(species_ref, na):
     row = lax.broadcasted_iota(jnp.int32, (na, 128), 0)
     species = jnp.zeros((na, 128), jnp.int32)
     for a in range(na):
         species = jnp.where(row == a, species_ref[0, 0, a], species)
-    first = species == 0
-    first_f = jnp.where(first, 1.0, 0.0).astype(f32)
+    return species == 0
+
+
+def prepare_kernel(
+    ni, nrad, npts, na,
+    species_ref, d_ref, ae_core_ref, ps_core_ref, radial_ref, lhs_ref, line_ref, lhs32,
+):
+    f32, bf16 = jnp.float32, jnp.bfloat16
+    first_f = jnp.where(first_species(species_ref, na), 1.0, 0.0).astype(f32)
     second_f = 1.0 - first_f
-
     lhs32[...] = jnp.zeros_like(lhs32)
     for i in range(ni):
         d = d_ref[:, ni * i : ni * (i + 1)]
@@ -126,21 +127,61 @@
             at = 2 * ROW * block
             lhs32[here, at : at + ni] = part * first_f[:, :ni]
             lhs32[here, at + ROW : at + ROW + ni] = part * second_f[:, :ni]
-    lhs = lhs32[:, 0 : 6 * ROW].astype(bf16)
-
-    longest = max(high - low for _, low, high in units)
-    cores[0:2, 0:nrad] = ae_core_ref[...]
-    cores[2:4, 0:nrad] = ps_core_ref[...]
+    lhs_ref[...] = lhs32[:, 0 : 6 * ROW].astype(bf16)
+
+    width = line_ref.shape[1]
+    line_ref[0:2, 0:nrad] = ae_core_ref[...]
+    line_ref[2:4, 0:nrad] = ps_core_ref[...]
+    line_ref[4:RADIAL, 0:nrad] = jnp.ones((RADIAL - 4, nrad), f32)
+    line_ref[RADIAL:, 0:nrad] = radial_ref[...]
     reach = nrad
-    while reach < longest:
-        more = min(reach, longest - reach)
-        cores[0:4, reach : reach + more] = cores[0:4, 0:more]
+    while reach < width:
+        more = min(reach, width - reach)
+        line_ref[:, reach : reach + more] = line_ref[:, 0:more]
         reach += more
+    line_ref[RADIAL:, npts:] = jnp.zeros((8, width - npts), f32)
+
+
+def prepare(species, matrices, ae_core, ps_core, npts):
+    na, pairs = matrices.shape
+    ni = math.isqrt(pairs)
+    nrad = ae_core.shape[1]
+    width = -(-npts // 128) * 128
+    vmem = pl.BlockSpec(memory_space=pltpu.VMEM)
+    smem = pl.BlockSpec(memory_space=pltpu.SMEM)
+    f32, bf16 = jnp.float32, jnp.bfloat16
+    return pl.pallas_call(
+        functools.partial(prepare_kernel, ni, nrad, npts, na),
+        out_shape=(
+            jax.ShapeDtypeStruct((na * ni, 6 * ROW), bf16),
+            jax.ShapeDtypeStruct((RADIAL + 8, width), f32),
+        ),
+        in_specs=[smem] + [vmem] * 4,
+        out_specs=(vmem,) * 2,
+        scratch_shapes=[pltpu.VMEM((na * ni, 256), f32)],
+        compiler_params=pltpu.CompilerParams(vmem_limit_bytes=8 << 20),
+        cost_estimate=pl.CostEstimate(flops=1 << 31, transcendentals=0, bytes_accessed=6 << 20),
+        name="prepare",
+    )(species, matrices, ae_core, ps_core, jnp.asarray(radial_table(nrad)))
+
+
+def atoms_kernel(
+    ni, nrad, npts, na, table, runs, has_sums, carried,
+    count_ref, species_ref, x_ref, lhs_ref, line_ref, *refs,
+):
+    f32, bf16 = jnp.float32, jnp.bfloat16
+    if has_sums:
+        h_in_ref, e_in_ref, *refs = refs
+    carry_in, (h_ref, e_ref, *refs) = refs[:carried], refs[carried:]
+    carry_out, (total, *scratch) = refs[:carried], refs[carried:]
+    for source, target in zip(carry_in, carry_out):
+        target[...] = source[...]
+    first = first_species(species_ref, na)
+    row = lax.broadcasted_iota(jnp.int32, (na, 128), 0)
 
     e_sum = jnp.zeros((na, 128), f32)
-    for u, (table, low, high) in enumerate(units):
+    for u, (low, high) in enumerate(runs):
         waves, packed, rho, part_q = scratch[4 * u : 4 * u + 4]
-        x_ref = (ae_ref, ps_ref)[table]
         size, live = high - low, min(high, npts) - low
         tail = live // 128 * 128
         if tail < size:
@@ -154,11 +195,13 @@
         x1 = x.astype(bf16)
         x2 = (x - x1.astype(f32)).astype(bf16)
         packed[...] = jnp.concatenate([x1, x2], axis=0)
-        mixed = jnp.dot(lhs, jnp.concatenate([x1, x2, x1], axis=0), preferred_element_type=f32)
+        mixed = jnp.dot(
+            lhs_ref[...], jnp.concatenate([x1, x2, x1], axis=0), preferred_element_type=f32
+        )
         n = jnp.where(
             pick,
-            cores[2 * table : 2 * table + 1, 0:size],
-            cores[2 * table + 1 : 2 * table + 2, 0:size],
+            line_ref[2 * table : 2 * table + 1, low:high],
+            line_ref[2 * table + 1 : 2 * table + 2, low:high],
         )
         for i in range(ni):
             own = jnp.where(pick, x[i : i + 1], x[ROW + i : ROW + i + 1])
@@ -167,7 +210,7 @@
 
         scale = (-1.0 if table else 1.0) * 4.0 * math.pi * nrad / npts
         n = rho[...]
-        radial = radial_ref[:, low:high]
+        radial = line_ref[RADIAL:, low:high]
         weight = radial[0:1] * scale
         up, mid, down = radial[1:2], radial[2:3], radial[3:4]
         slope = up * pltpu.roll(n, size - 1, 1) + mid * n + down * pltpu.roll(n, 1, 1)
@@ -178,7 +221,7 @@
         part_q[...] = (slope * e_s) * (2.0 * weight)
         q = part_q[...]
         g = e_n * weight + mid * q
-        g = g + radial[5:6] * pltpu.roll(q, 1, 1) + radial[6:7] * pltpu.roll(q, size - 1, 1)
+        g = g + radial[4:5] * pltpu.roll(q, 1, 1) + radial[5:6] * pltpu.roll(q, size - 1, 1)
         rho[...] = g
         g = rho[...]
         x = waves[...]
@@ -204,33 +247,28 @@
         value = both[:, 0 : 2 * ROW] + both[:, 2 * ROW : 4 * ROW]
         value = jnp.where(first[:, :ni], value[:, 0:ni], value[:, ROW : ROW + ni])
         here = slice(ni * i, ni * (i + 1))
-        h_ref[:, here] = h_in_ref[:, here] + jnp.where(live[:, :ni], value, 0.0)
+        value = jnp.where(live[:, :ni], value, 0.0)
+        h_ref[:, here] = h_in_ref[:, here] + value if has_sums else value
     energy = jnp.sum(e_sum, axis=1, keepdims=True)
     energy = jnp.where(live[:, :1], energy, 0.0)
     diagonal = lax.broadcasted_iota(jnp.int32, (na, na), 0) == lax.broadcasted_iota(
         jnp.int32, (na, na), 1
     )
-    e_ref[...] = e_in_ref[...] + jnp.sum(jnp.where(diagonal, energy, 0.0), axis=0, keepdims=True)
-
-
-def atom_terms(units, sums, count, species, matrices, ae, ps, ae_core, ps_core):
-    na, pairs = matrices.shape
-    ni, npts = ae.shape[1], ae.shape[2]
-    nrad = ae_core.shape[1]
-    width = -(-npts // 128) * 128
-    radial = radial_table(nrad, npts, width)
-    radial[5] = np.roll(radial[1], 1)
-    radial[6] = np.roll(radial[3], -1)
+    energy = jnp.sum(jnp.where(diagonal, energy, 0.0), axis=0, keepdims=True)
+    e_ref[...] = e_in_ref[...] + energy if has_sums else energy
+
+
+def atom_terms(table, count, species, x, lhs, line, nrad, sums=(), carry=()):
+    _, ni, npts = x.shape
+    na = lhs.shape[0] // ni
+    width = line.shape[1]
+    cut = math.lcm(nrad, 128)
+    runs = [(low, min(low + cut, width)) for low in range(0, width, cut)]
     vmem = pl.BlockSpec(memory_space=pltpu.VMEM)
     smem = pl.BlockSpec(memory_space=pltpu.SMEM)
     f32, bf16 = jnp.float32, jnp.bfloat16
-    points = sum(high - low for _, low, high in units)
-    scratch = [
-        pltpu.VMEM((na * ni, 256), f32),
-        pltpu.VMEM((8, max(high - low for _, low, high in units)), f32),
-        pltpu.VMEM((2 * na * ni, 4 * ROW), f32),
-    ]
-    for _, low, high in units:
+    scratch = [pltpu.VMEM((2 * na * ni, 4 * ROW), f32)]
+    for low, high in runs:
         scratch += [
             pltpu.VMEM((2 * ROW, high - low), f32),
             pltpu.VMEM((4 * ROW, high - low), bf16),
@@ -238,20 +276,21 @@
             pltpu.VMEM((na, high - low), f32),
         ]
     return pl.pallas_call(
-        functools.partial(atoms_kernel, ni, nrad, npts, na, units),
+        functools.partial(atoms_kernel, ni, nrad, npts, na, table, runs, bool(sums), len(carry)),
         out_shape=(
-            jax.ShapeDtypeStruct((na, pairs), f32),
+            jax.ShapeDtypeStruct((na, ni * ni), f32),
             jax.ShapeDtypeStruct((1, na), f32),
+            *(jax.ShapeDtypeStruct(c.shape, c.dtype) for c in carry),
         ),
-        in_specs=[smem, smem] + [vmem] * 8,
-        out_specs=(vmem, vmem),
+        in_specs=[smem, smem] + [vmem] * (3 + len(sums) + len(carry)),
+        out_specs=(vmem,) * (2 + len(carry)),
         scratch_shapes=scratch,
-        compiler_params=pltpu.CompilerParams(vmem_limit_bytes=40 << 20),
+        compiler_params=pltpu.CompilerParams(vmem_limit_bytes=32 << 20),
         cost_estimate=pl.CostEstimate(
-            flops=4 * na * ni * ni * points, transcendentals=na * points * 10, bytes_accessed=2 << 20
+            flops=4 * na * ni * ni * npts, transcendentals=na * npts * 10, bytes_accessed=2 << 20
         ),
         name="atoms",
-    )(count, species, matrices, ae, ps, ae_core, ps_core, jnp.asarray(radial), *sums)
+    )(count, species, x, lhs, line, *sums, *carry)
 
 
 def upsampling(cells, halo):
@@ -337,8 +376,7 @@
         v_ref[x] = e_n[here] - (2.0 * inv * inv) * (change[here] + (after - before))
 
 
-def grid_terms(columns, nx, ny, nz):
-    left, right = grid_tables(nx, ny, nz)
+def grid_terms(columns, left, right, nx, ny, nz):
     fx, fy, fz = 2 * nx, 2 * ny, 2 * nz
     vmem = pl.BlockSpec(memory_space=pltpu.VMEM)
     fine = jax.ShapeDtypeStruct((fx, fy, fz), jnp.float32)
@@ -352,10 +390,10 @@
             flops=300 * fx * fy * fz, transcendentals=10 * fx * fy * fz, bytes_accessed=2 << 20
         ),
         name="grid",
-    )(columns, jnp.asarray(left, jnp.bfloat16), jnp.asarray(right, jnp.bfloat16))
-
-
-def with_halo(cells, axis, dim, width, work, sums):
+    )(columns, left, right)
+
+
+def with_halo(cells, axis, dim, width, work, later=()):
     count = lax.axis_size(axis)
     even = lax.axis_index(axis) % 2 == 0
     head = lax.slice_in_dim(cells, 0, width, axis=dim)
@@ -364,14 +402,9 @@
     outer = [(i, (i + 1 if i % 2 else i - 1) % count) for i in range(count)]
     first = lax.ppermute(jnp.where(even, tail, head), axis, inner)
     second = lax.ppermute(jnp.where(even, head, tail), axis, outer)
-    sums = work(sums)
-    first, second, sums = lax.optimization_barrier((first, second, sums))
-    return (
-        jnp.concatenate(
-            [jnp.where(even, second, first), cells, jnp.where(even, first, second)], axis=dim
-        ),
-        sums,
-    )
+    second, first, done, later = lax.optimization_barrier((second, first, work(), later))
+    low, high = jnp.where(even, second, first), jnp.where(even, first, second)
+    return jnp.concatenate([low, cells, high], axis=dim), done, later
 
 
 def shards(
@@ -385,25 +418,27 @@
     smooth_core,
 ):
     slots, pairs = density_matrix.shape[2:]
-    owned = (
-        atom_count,
-        atom_species,
-        density_matrix.reshape(slots, pairs),
+    nrad, npts = core_density.shape[1], partial_waves.shape[2]
+    block = coarse_density.shape
+    weights = tuple(jnp.asarray(w, jnp.bfloat16) for w in grid_tables(*block))
+    cells, (lhs, line), partial_waves = with_halo(
+        coarse_density, "gy", 1, 2,
+        lambda: prepare(
+            atom_species, density_matrix.reshape(slots, pairs), core_density, smooth_core, npts
+        ),
         partial_waves,
+    )
+    cells, (*sums, left, right), smooth_waves = with_halo(
+        cells, "gx", 0, 2,
+        lambda: atom_terms(0, atom_count, atom_species, partial_waves, lhs, line, nrad, (), weights),
         smooth_waves,
-        core_density,
-        smooth_core,
-    )
-    sums = (jnp.zeros((slots, pairs), jnp.float32), jnp.zeros((1, slots), jnp.float32))
-    cells = coarse_density
-    runs = [(), ((0, 0, 3200), (0, 3200, 5120)), ((1, 0, 3200), (1, 3200, 5120))]
-    for (axis, dim), units in zip((("gy", 1), ("gx", 0), ("gz", 2)), runs):
-        cells, sums = with_halo(
-            cells, axis, dim, 2, lambda s: atom_terms(units, s, *owned) if units else s, sums
-        )
-    placed, placed_energy = sums
+    )
+    cells, (placed, placed_energy), _ = with_halo(
+        cells, "gz", 2, 2,
+        lambda: atom_terms(1, atom_count, atom_species, smooth_waves, lhs, line, nrad, sums),
+    )
     columns = cells.transpose(1, 0, 2).reshape(-1, cells.shape[2])
-    potential, energy_density = grid_terms(columns, *coarse_density.shape)
+    potential, energy_density = grid_terms(columns, left, right, *block)
     return (
         potential,
         energy_density,

time: 34.2 us -> 32.1 us (0.939)
  local copies, waits for them, and re-layouts: 3.95 us -> 1.9 us
    unnamed x20, local copies, waits for them, and re-layouts: 3.93 us -> 1.39 us
    optimization_barrier x0 -> x2, local copies, waits for them, and re-layouts: none -> 0.49 us  [with_halo(): lax.optimization_barrier((second, first, work(), later))]
    pallas_call x2 -> x3, Pallas kernels: 11.3 us -> 11.3 us  [the longest x2 10.2 us: atom_terms(): pl.pallas_call(functools.partial(atoms_kernel, ni, nrad, npts, na, table,...]
  transfers between devices with their start and end apart: 6 -> 6, of which waited for: 0 -> 0; matrix products, arithmetic and copies ran while one was open for 5% -> 0% of each run, Pallas kernels for 33% -> 36%
where the time goes in v3:
time: 32.1 us; the launch traced here: 31.8 us
  starting transfers between devices  15.2 us (47%)
  Pallas kernels  13 us (40%)
  local copies, waits for them, and re-layouts  1.9 us (6%)
  between operations  1.53 us (5%)
    ppermute x3, starting transfers between devices, with_halo(): second = lax.ppermute(jnp.where(even, head, tail), axis, outer)  15.1 us
    pallas_call x2, Pallas kernels, atom_terms(): pl.pallas_call(functools.partial(atoms_kernel, ni, nrad, npts, na, table,...  10.2 us
    pallas_call x1, Pallas kernels, grid_terms(): pl.pallas_call(functools.partial(grid_kernel, fx, fy, fz), out_shape=(fin...  1.67 us
    unnamed x20, local copies, waits for them, and re-layouts  1.39 us
    pallas_call x1, Pallas kernels, prepare(): pl.pallas_call(functools.partial(prepare_kernel, ni, nrad, npts, na), out...  1.05 us
  transfers between devices with their start and end apart: 6, of which 0 were waited for; matrix products, arithmetic and copies ran while one was open for 0% of the time, Pallas kernels for 36%

profile of v3, /device:TPU:1, one launch (start us, length us, event | category | flops | bytes accessed | tf_op | source)
XLA Modules:
  0.0 31.8 jit_solution(8998611446056334462)
XLA Ops:
  0.6 0.0 copy-start.9
  0.6 0.0 copy-start.3
  0.7 0.7 %copy-done.9 = f32[4,8,64]{2,1,0:T(8,128)S(1)} copy-done((f32[4,8,64]{2,1,0:T(8,128)S(1)}, f32[4,8,64]{2,1,0:T(8,128)}, u32[]{:S(2)}) %copy-start.9) | copy-done | bytes 8216
  1.3 0.0 copy-start.6
  1.4 8.4 %collective-permute-start = (f32[4,2,64]{2,1,0:T(2,128)S(1)}, f32[4,2,64]{2,1,0:T(2,128)S(1)}, u32[]{:S(2)}, u32[]{:S(2)}) collective-permute-start(f32[4,2,64]{2,1,0:T(2,128)S(1)} %get-tuple-element.65), channel_id=1, source_target_pairs={{0,12},{4,8},{8,4},{12,0},{1,13},{5,9},{9,5},{13,1},{2,14},{6,10},... | collective-permute-start | bytes 6152 | tf_op jit(solution)/shard_map/ppermute | solution.py:404
  9.7 0.0 copy-start.5
  9.7 0.0 copy-start.2
  9.8 0.0 copy-start.4
  9.8 0.0 collective-permute-start.1
  9.8 0.0 copy-done.3
  9.8 0.0 copy-done.6
  9.8 0.6 %copy-done.5 = f32[2,100]{1,0:T(2,128)S(1)} copy-done((f32[2,100]{1,0:T(2,128)S(1)}, f32[2,100]{1,0:T(2,128)}, u32[]{:S(2)}) %copy-start.5) | copy-done | bytes 824
  10.4 0.0 copy-done.2
  10.4 0.0 copy-done.4
  10.5 0.0 copy-start.7
  10.5 1.0 %prepare.1 = (bf16[288,144]{1,0:T(8,128)(2,1)S(1)}, f32[16,5120]{1,0:T(8,128)S(1)}) custom-call(s32[1,1,16]{2,1,0:T(1,128)S(1)} %copy-done.2, f32[16,324]{1,0:T(8,128)S(1)} %bitcast.13, f32[2,100]{1,0:T(2,128)S(1)} %copy-done.4, f32[2,100]{1,0:T(2,128)S(1)} %copy-done.5, f32[8,100]{1,0:T(8,128)S(1)} %copy-done.6), custom_call_target="tpu_custom_call" | custom-call | flops 2147483648 | bytes 6291456 | tf_op jit(solution)/shard_map/prepare/pallas_call | solution.py:153
  12.2 0.0 collective-permute-done
  12.2 0.0 collective-permute-done.1
  12.2 0.0 copy-done.7
  12.2 0.0 copy-start
  12.2 0.2 copy.15.x_ref
  12.5 0.0 copy-start.1
  12.5 5.0 %collective-permute-start.2 = (f32[2,12,64]{2,1,0:T(8,128)S(1)}, f32[2,12,64]{2,1,0:T(8,128)S(1)}, u32[]{:S(2)}, u32[]{:S(2)}) collective-permute-start(f32[2,12,64]{2,1,0:T(8,128)S(1)} %get-tuple-element.63), channel_id=1, source_target_pairs={{0,240},{16,32},{32,16},{48,64},{64,48},{80,96},{96,80},{112,128},... | collective-permute-start | bytes 18440 | tf_op jit(solution)/shard_map/ppermute | solution.py:404
  17.6 0.0 copy-start.8
  17.6 0.0 collective-permute-start.3
  17.6 0.0 copy-done
  17.6 0.0 copy-done.1
  17.6 4.9 %atoms.2 = (f32[16,324]{1,0:T(8,128)S(1)}, f32[1,16]{1,0:T(1,128)S(1)}, bf16[528,288]{1,0:T(8,128)(2,1)S(1)}, bf16[68,512]{1,0:T(8,128)(2,1)S(1)}) custom-call(s32[1,1]{1,0:T(1,128)S(6)} %copy.20.count_ref, s32[1,1,16]{2,1,0:T(1,128)S(1)} %copy-done.2, f32[2,18,5000]{2,1,0:T(8,128)S(1)} %copy.15.x_ref, bf16[288,144]{1,0:T(8,128)(2,1)S(1)} %get-tuple-element.35.lhs_ref, ...), custom_call_target="tpu_custom_call" | custom-call | flops 103680000 | bytes 2097152 | tf_op jit(solution)/shard_map/atoms/pallas_call | solution.py:278
  22.5 0.0 collective-permute-done.2
  22.5 0.0 collective-permute-done.3
  22.5 0.0 copy-done.8
  22.5 0.2 copy.16.x_ref
  22.8 0.1 slice_select_fusion
  22.9 1.7 %collective-permute-start.4 = (f32[8,12,2]{2,1,0:T(8,128)S(1)}, f32[8,12,2]{2,1,0:T(8,128)S(1)}, u32[]{:S(2)}, u32[]{:S(2)}) collective-permute-start(f32[8,12,2]{2,1,0:T(8,128)S(1)} %get-tuple-element.59), channel_id=1, source_target_pairs={{0,3},{1,2},{2,1},{3,0},{4,7},{5,6},{6,5},{7,4},{8,11},{9,10},{10,... | collective-permute-start | bytes 2312 | tf_op jit(solution)/shard_map/ppermute | solution.py:404
  24.6 0.0 collective-permute-start.5
  24.6 5.4 %atoms.3 = (f32[16,324]{1,0:T(8,128)}, f32[1,16]{1,0:T(1,128)}) custom-call(s32[1,1]{1,0:T(1,128)S(6)} %copy.20.count_ref, s32[1,1,16]{2,1,0:T(1,128)S(1)} %copy-done.2, f32[2,18,5000]{2,1,0:T(8,128)S(1)} %copy.16.x_ref, bf16[288,144]{1,0:T(8,128)(2,1)S(1)} %get-tuple-element.35.lhs_ref, f32[16,5120]{1,0:T(8,128)S(1)} %get-tuple-element.36.line_ref, ...), custom_call_target="tpu_custom_call" | custom-call | flops 103680000 | bytes 2097152 | tf_op jit(solution)/shard_map/atoms/pallas_call | solution.py:278
  30.0 0.0 collective-permute-done.4
  30.0 0.0 collective-permute-done.5
  30.0 0.1 maximum_bitcast_fusion
  30.2 1.7 %grid.1 = (f32[8,16,128]{2,1,0:T(8,128)}, f32[8,16,128]{2,1,0:T(8,128)}) custom-call(f32[96,68]{1,0:T(8,128)S(1)} %bitcast.12, bf16[528,288]{1,0:T(8,128)(2,1)S(1)} %get-tuple-element.50.left_ref, bf16[68,512]{1,0:T(8,128)(2,1)S(1)} %get-tuple-element.51.right_ref), custom_call_target="tpu_custom_call" | custom-call | flops 4915200 | bytes 2097152 | tf_op jit(solution)/shard_map/grid/pallas_call | solution.py:383
  (8 shorter events, 0.1 us)
Async XLA Ops:
  0.6 0.7 %copy-start.9 = (f32[4,8,64]{2,1,0:T(8,128)S(1)}, f32[4,8,64]{2,1,0:T(8,128)}, u32[]{:S(2)}) copy-start(f32[4,8,64]{2,1,0:T(8,128)} %param.11) | copy-start | bytes 24580
  0.6 9.1 %copy-start.3 = (f32[1,1,16,324]{3,2,1,0:T(8,128)S(1)}, f32[1,1,16,324]{3,2,1,0:T(8,128)}, u32[]{:S(2)}) copy-start(f32[1,1,16,324]{3,2,1,0:T(8,128)} %param.14) | copy-start | bytes 62212
  1.3 8.4 %copy-start.6 = (f32[8,100]{1,0:T(8,128)S(1)}, f32[8,100]{1,0:T(8,128)}, u32[]{:S(2)}) copy-start(f32[8,100]{1,0:T(8,128)} %constant.42.clone.radial_ref) | copy-start | bytes 9604
  1.4 10.8 %collective-permute-start = (f32[4,2,64]{2,1,0:T(2,128)S(1)}, f32[4,2,64]{2,1,0:T(2,128)S(1)}, u32[]{:S(2)}, u32[]{:S(2)}) collective-permute-start(f32[4,2,64]{2,1,0:T(2,128)S(1)} %get-tuple-element.65), channel_id=1, source_target_pairs={{0,12},{4,8},{8,4},{12,0},{1,13},{5,9},{9,5},{13,1},{2,14},{6,10},... | collective-permute-start | bytes 6152 | tf_op jit(solution)/shard_map/ppermute | solution.py:404
  9.7 0.7 %copy-start.5 = (f32[2,100]{1,0:T(2,128)S(1)}, f32[2,100]{1,0:T(2,128)}, u32[]{:S(2)}) copy-start(f32[2,100]{1,0:T(2,128)} %ps_core_ref.1) | copy-start | bytes 2404
  9.7 0.7 %copy-start.2 = (s32[1,1,16]{2,1,0:T(1,128)S(1)}, s32[1,1,16]{2,1,0:T(1,128)}, u32[]{:S(2)}) copy-start(s32[1,1,16]{2,1,0:T(1,128)} %species_ref.5) | copy-start | bytes 196
  9.8 0.7 %copy-start.4 = (f32[2,100]{1,0:T(2,128)S(1)}, f32[2,100]{1,0:T(2,128)}, u32[]{:S(2)}) copy-start(f32[2,100]{1,0:T(2,128)} %ae_core_ref.1) | copy-start | bytes 2404
  9.8 2.4 %collective-permute-start.1 = (f32[4,2,64]{2,1,0:T(2,128)S(1)}, f32[4,2,64]{2,1,0:T(2,128)S(1)}, u32[]{:S(2)}, u32[]{:S(2)}) collective-permute-start(f32[4,2,64]{2,1,0:T(2,128)S(1)} %get-tuple-element.64), channel_id=1, source_target_pairs={{0,4},{4,0},{8,12},{12,8},{1,5},{5,1},{9,13},{13,9},{2,6},{6,2},{1... | collective-permute-start | bytes 6152 | tf_op jit(solution)/shard_map/ppermute | solution.py:403
  10.5 1.7 %copy-start.7 = (f32[2,18,5000]{2,0,1:T(2,128)S(1)}, f32[2,18,5000]{2,0,1:T(2,128)}, u32[]{:S(2)}) copy-start(f32[2,18,5000]{2,0,1:T(2,128)} %param.15) | copy-start | bytes 2160004
  12.2 5.3 %copy-start = (bf16[528,288]{1,0:T(8,128)(2,1)S(1)}, bf16[528,288]{1,0:T(8,128)(2,1)}, u32[]{:S(2)}) copy-start(bf16[528,288]{1,0:T(8,128)(2,1)} %constant.40.clone.refs_0_) | copy-start | bytes 912388
  12.5 5.1 %copy-start.1 = (bf16[68,512]{1,0:T(8,128)(2,1)S(1)}, bf16[68,512]{1,0:T(8,128)(2,1)}, u32[]{:S(2)}) copy-start(bf16[68,512]{1,0:T(8,128)(2,1)} %constant.41.clone.refs_1_) | copy-start | bytes 208900
  12.5 9.9 %collective-permute-start.2 = (f32[2,12,64]{2,1,0:T(8,128)S(1)}, f32[2,12,64]{2,1,0:T(8,128)S(1)}, u32[]{:S(2)}, u32[]{:S(2)}) collective-permute-start(f32[2,12,64]{2,1,0:T(8,128)S(1)} %get-tuple-element.63), channel_id=1, source_target_pairs={{0,240},{16,32},{32,16},{48,64},{64,48},{80,96},{96,80},{112,128},... | collective-permute-start | bytes 18440 | tf_op jit(solution)/shard_map/ppermute | solution.py:404
  17.6 4.9 %copy-start.8 = (f32[2,18,5000]{2,0,1:T(2,128)S(1)}, f32[2,18,5000]{2,0,1:T(2,128)}, u32[]{:S(2)}) copy-start(f32[2,18,5000]{2,0,1:T(2,128)} %param.16) | copy-start | bytes 2160004
  17.6 4.9 %collective-permute-start.3 = (f32[2,12,64]{2,1,0:T(8,128)S(1)}, f32[2,12,64]{2,1,0:T(8,128)S(1)}, u32[]{:S(2)}, u32[]{:S(2)}) collective-permute-start(f32[2,12,64]{2,1,0:T(8,128)S(1)} %get-tuple-element.62), channel_id=1, source_target_pairs={{0,16},{16,0},{32,48},{48,32},{64,80},{80,64},{96,112},{112,96},{1... | collective-permute-start | bytes 18440 | tf_op jit(solution)/shard_map/ppermute | solution.py:403
  22.9 7.1 %collective-permute-start.4 = (f32[8,12,2]{2,1,0:T(8,128)S(1)}, f32[8,12,2]{2,1,0:T(8,128)S(1)}, u32[]{:S(2)}, u32[]{:S(2)}) collective-permute-start(f32[8,12,2]{2,1,0:T(8,128)S(1)} %get-tuple-element.59), channel_id=1, source_target_pairs={{0,3},{1,2},{2,1},{3,0},{4,7},{5,6},{6,5},{7,4},{8,11},{9,10},{10,... | collective-permute-start | bytes 2312 | tf_op jit(solution)/shard_map/ppermute | solution.py:404
  24.6 5.4 %collective-permute-start.5 = (f32[8,12,2]{2,1,0:T(8,128)S(1)}, f32[8,12,2]{2,1,0:T(8,128)S(1)}, u32[]{:S(2)}, u32[]{:S(2)}) collective-permute-start(f32[8,12,2]{2,1,0:T(8,128)S(1)} %get-tuple-element.58), channel_id=1, source_target_pairs={{0,1},{1,0},{2,3},{3,2},{4,5},{5,4},{6,7},{7,6},{8,9},{9,8},{10,11... | collective-permute-start | bytes 2312 | tf_op jit(solution)/shard_map/ppermute | solution.py:403

commit v4 on v3

--- a/solution.py
+++ b/solution.py
@@ -262,8 +262,7 @@
     _, ni, npts = x.shape
     na = lhs.shape[0] // ni
     width = line.shape[1]
-    cut = math.lcm(nrad, 128)
-    runs = [(low, min(low + cut, width)) for low in range(0, width, cut)]
+    runs = [(0, width)]
     vmem = pl.BlockSpec(memory_space=pltpu.VMEM)
     smem = pl.BlockSpec(memory_space=pltpu.SMEM)
     f32, bf16 = jnp.float32, jnp.bfloat16

time: 32.1 us -> 31.8 us (level)
  transfers between devices with their start and end apart: 6 -> 6, of which waited for: 0 -> 0; matrix products, arithmetic and copies ran while one was open for 0% -> 0% of each run, Pallas kernels for 36% -> 35%
where the time goes in v4:
time: 31.8 us; the launch traced here: 31.5 us
  starting transfers between devices  15.1 us (47%)
  Pallas kernels  12.7 us (40%)
  local copies, waits for them, and re-layouts  1.9 us (6%)
  between operations  1.52 us (5%)
    ppermute x3, starting transfers between devices, with_halo(): second = lax.ppermute(jnp.where(even, head, tail), axis, outer)  15.1 us
    pallas_call x2, Pallas kernels, atom_terms(): pl.pallas_call(functools.partial(atoms_kernel, ni, nrad, npts, na, table,...  9.96 us
    pallas_call x1, Pallas kernels, grid_terms(): pl.pallas_call(functools.partial(grid_kernel, fx, fy, fz), out_shape=(fin...  1.67 us
    unnamed x20, local copies, waits for them, and re-layouts  1.39 us
    pallas_call x1, Pallas kernels, prepare(): pl.pallas_call(functools.partial(prepare_kernel, ni, nrad, npts, na), out...  1.05 us
  transfers between devices with their start and end apart: 6, of which 0 were waited for; matrix products, arithmetic and copies ran while one was open for 0% of the time, Pallas kernels for 35%

profile of v4, /device:TPU:1, one launch (start us, length us, event | category | flops | bytes accessed | tf_op | source)
XLA Modules:
  0.0 31.5 jit_solution(592292970432814152)
XLA Ops:
  0.6 0.0 copy-start.9
  0.6 0.0 copy-start.3
  0.7 0.7 %copy-done.9 = f32[4,8,64]{2,1,0:T(8,128)S(1)} copy-done((f32[4,8,64]{2,1,0:T(8,128)S(1)}, f32[4,8,64]{2,1,0:T(8,128)}, u32[]{:S(2)}) %copy-start.9) | copy-done | bytes 8216
  1.3 0.0 copy-start.6
  1.4 8.4 %collective-permute-start = (f32[4,2,64]{2,1,0:T(2,128)S(1)}, f32[4,2,64]{2,1,0:T(2,128)S(1)}, u32[]{:S(2)}, u32[]{:S(2)}) collective-permute-start(f32[4,2,64]{2,1,0:T(2,128)S(1)} %get-tuple-element.65), channel_id=1, source_target_pairs={{0,12},{4,8},{8,4},{12,0},{1,13},{5,9},{9,5},{13,1},{2,14},{6,10},... | collective-permute-start | bytes 6152 | tf_op jit(solution)/shard_map/ppermute | solution.py:403
  9.7 0.0 copy-start.5
  9.7 0.0 copy-start.2
  9.8 0.0 copy-start.4
  9.8 0.0 collective-permute-start.1
  9.8 0.0 copy-done.3
  9.8 0.0 copy-done.6
  9.8 0.6 %copy-done.5 = f32[2,100]{1,0:T(2,128)S(1)} copy-done((f32[2,100]{1,0:T(2,128)S(1)}, f32[2,100]{1,0:T(2,128)}, u32[]{:S(2)}) %copy-start.5) | copy-done | bytes 824
  10.4 0.0 copy-done.2
  10.4 0.0 copy-done.4
  10.5 0.0 copy-start.7
  10.5 1.0 %prepare.1 = (bf16[288,144]{1,0:T(8,128)(2,1)S(1)}, f32[16,5120]{1,0:T(8,128)S(1)}) custom-call(s32[1,1,16]{2,1,0:T(1,128)S(1)} %copy-done.2, f32[16,324]{1,0:T(8,128)S(1)} %bitcast.13, f32[2,100]{1,0:T(2,128)S(1)} %copy-done.4, f32[2,100]{1,0:T(2,128)S(1)} %copy-done.5, f32[8,100]{1,0:T(8,128)S(1)} %copy-done.6), custom_call_target="tpu_custom_call" | custom-call | flops 2147483648 | bytes 6291456 | tf_op jit(solution)/shard_map/prepare/pallas_call | solution.py:153
  12.2 0.0 collective-permute-done
  12.2 0.0 collective-permute-done.1
  12.2 0.0 copy-done.7
  12.2 0.0 copy-start
  12.2 0.2 copy.15.x_ref
  12.5 0.0 copy-start.1
  12.5 5.0 %collective-permute-start.2 = (f32[2,12,64]{2,1,0:T(8,128)S(1)}, f32[2,12,64]{2,1,0:T(8,128)S(1)}, u32[]{:S(2)}, u32[]{:S(2)}) collective-permute-start(f32[2,12,64]{2,1,0:T(8,128)S(1)} %get-tuple-element.63), channel_id=1, source_target_pairs={{0,240},{16,32},{32,16},{48,64},{64,48},{80,96},{96,80},{112,128},... | collective-permute-start | bytes 18440 | tf_op jit(solution)/shard_map/ppermute | solution.py:403
  17.6 0.0 copy-start.8
  17.6 0.0 collective-permute-start.3
  17.6 0.0 copy-done
  17.6 0.0 copy-done.1
  17.6 4.8 %atoms.2 = (f32[16,324]{1,0:T(8,128)S(1)}, f32[1,16]{1,0:T(1,128)S(1)}, bf16[528,288]{1,0:T(8,128)(2,1)S(1)}, bf16[68,512]{1,0:T(8,128)(2,1)S(1)}) custom-call(s32[1,1]{1,0:T(1,128)S(6)} %copy.20.count_ref, s32[1,1,16]{2,1,0:T(1,128)S(1)} %copy-done.2, f32[2,18,5000]{2,1,0:T(8,128)S(1)} %copy.15.x_ref, bf16[288,144]{1,0:T(8,128)(2,1)S(1)} %get-tuple-element.35.lhs_ref, ...), custom_call_target="tpu_custom_call" | custom-call | flops 103680000 | bytes 2097152 | tf_op jit(solution)/shard_map/atoms/pallas_call | solution.py:277
  22.3 0.0 collective-permute-done.2
  22.3 0.0 collective-permute-done.3
  22.3 0.0 copy-done.8
  22.4 0.2 copy.16.x_ref
  22.6 0.1 slice_select_fusion
  22.7 1.7 %collective-permute-start.4 = (f32[8,12,2]{2,1,0:T(8,128)S(1)}, f32[8,12,2]{2,1,0:T(8,128)S(1)}, u32[]{:S(2)}, u32[]{:S(2)}) collective-permute-start(f32[8,12,2]{2,1,0:T(8,128)S(1)} %get-tuple-element.59), channel_id=1, source_target_pairs={{0,3},{1,2},{2,1},{3,0},{4,7},{5,6},{6,5},{7,4},{8,11},{9,10},{10,... | collective-permute-start | bytes 2312 | tf_op jit(solution)/shard_map/ppermute | solution.py:403
  24.5 0.0 collective-permute-start.5
  24.5 5.2 %atoms.3 = (f32[16,324]{1,0:T(8,128)}, f32[1,16]{1,0:T(1,128)}) custom-call(s32[1,1]{1,0:T(1,128)S(6)} %copy.20.count_ref, s32[1,1,16]{2,1,0:T(1,128)S(1)} %copy-done.2, f32[2,18,5000]{2,1,0:T(8,128)S(1)} %copy.16.x_ref, bf16[288,144]{1,0:T(8,128)(2,1)S(1)} %get-tuple-element.35.lhs_ref, f32[16,5120]{1,0:T(8,128)S(1)} %get-tuple-element.36.line_ref, ...), custom_call_target="tpu_custom_call" | custom-call | flops 103680000 | bytes 2097152 | tf_op jit(solution)/shard_map/atoms/pallas_call | solution.py:277
  29.7 0.0 collective-permute-done.4
  29.7 0.0 collective-permute-done.5
  29.7 0.1 maximum_bitcast_fusion
  29.8 1.7 %grid.1 = (f32[8,16,128]{2,1,0:T(8,128)}, f32[8,16,128]{2,1,0:T(8,128)}) custom-call(f32[96,68]{1,0:T(8,128)S(1)} %bitcast.12, bf16[528,288]{1,0:T(8,128)(2,1)S(1)} %get-tuple-element.50.left_ref, bf16[68,512]{1,0:T(8,128)(2,1)S(1)} %get-tuple-element.51.right_ref), custom_call_target="tpu_custom_call" | custom-call | flops 4915200 | bytes 2097152 | tf_op jit(solution)/shard_map/grid/pallas_call | solution.py:382
  (8 shorter events, 0.1 us)
Async XLA Ops:
  0.6 0.7 %copy-start.9 = (f32[4,8,64]{2,1,0:T(8,128)S(1)}, f32[4,8,64]{2,1,0:T(8,128)}, u32[]{:S(2)}) copy-start(f32[4,8,64]{2,1,0:T(8,128)} %param.11) | copy-start | bytes 24580
  0.6 9.1 %copy-start.3 = (f32[1,1,16,324]{3,2,1,0:T(8,128)S(1)}, f32[1,1,16,324]{3,2,1,0:T(8,128)}, u32[]{:S(2)}) copy-start(f32[1,1,16,324]{3,2,1,0:T(8,128)} %param.14) | copy-start | bytes 62212
  1.3 8.4 %copy-start.6 = (f32[8,100]{1,0:T(8,128)S(1)}, f32[8,100]{1,0:T(8,128)}, u32[]{:S(2)}) copy-start(f32[8,100]{1,0:T(8,128)} %constant.42.clone.radial_ref) | copy-start | bytes 9604
  1.4 10.8 %collective-permute-start = (f32[4,2,64]{2,1,0:T(2,128)S(1)}, f32[4,2,64]{2,1,0:T(2,128)S(1)}, u32[]{:S(2)}, u32[]{:S(2)}) collective-permute-start(f32[4,2,64]{2,1,0:T(2,128)S(1)} %get-tuple-element.65), channel_id=1, source_target_pairs={{0,12},{4,8},{8,4},{12,0},{1,13},{5,9},{9,5},{13,1},{2,14},{6,10},... | collective-permute-start | bytes 6152 | tf_op jit(solution)/shard_map/ppermute | solution.py:403
  9.7 0.7 %copy-start.5 = (f32[2,100]{1,0:T(2,128)S(1)}, f32[2,100]{1,0:T(2,128)}, u32[]{:S(2)}) copy-start(f32[2,100]{1,0:T(2,128)} %ps_core_ref.1) | copy-start | bytes 2404
  9.7 0.7 %copy-start.2 = (s32[1,1,16]{2,1,0:T(1,128)S(1)}, s32[1,1,16]{2,1,0:T(1,128)}, u32[]{:S(2)}) copy-start(s32[1,1,16]{2,1,0:T(1,128)} %species_ref.5) | copy-start | bytes 196
  9.8 0.7 %copy-start.4 = (f32[2,100]{1,0:T(2,128)S(1)}, f32[2,100]{1,0:T(2,128)}, u32[]{:S(2)}) copy-start(f32[2,100]{1,0:T(2,128)} %ae_core_ref.1) | copy-start | bytes 2404
  9.8 2.4 %collective-permute-start.1 = (f32[4,2,64]{2,1,0:T(2,128)S(1)}, f32[4,2,64]{2,1,0:T(2,128)S(1)}, u32[]{:S(2)}, u32[]{:S(2)}) collective-permute-start(f32[4,2,64]{2,1,0:T(2,128)S(1)} %get-tuple-element.64), channel_id=1, source_target_pairs={{0,4},{4,0},{8,12},{12,8},{1,5},{5,1},{9,13},{13,9},{2,6},{6,2},{1... | collective-permute-start | bytes 6152 | tf_op jit(solution)/shard_map/ppermute | solution.py:402
  10.5 1.7 %copy-start.7 = (f32[2,18,5000]{2,0,1:T(2,128)S(1)}, f32[2,18,5000]{2,0,1:T(2,128)}, u32[]{:S(2)}) copy-start(f32[2,18,5000]{2,0,1:T(2,128)} %param.15) | copy-start | bytes 2160004
  12.2 5.3 %copy-start = (bf16[528,288]{1,0:T(8,128)(2,1)S(1)}, bf16[528,288]{1,0:T(8,128)(2,1)}, u32[]{:S(2)}) copy-start(bf16[528,288]{1,0:T(8,128)(2,1)} %constant.40.clone.refs_0_) | copy-start | bytes 912388
  12.5 5.1 %copy-start.1 = (bf16[68,512]{1,0:T(8,128)(2,1)S(1)}, bf16[68,512]{1,0:T(8,128)(2,1)}, u32[]{:S(2)}) copy-start(bf16[68,512]{1,0:T(8,128)(2,1)} %constant.41.clone.refs_1_) | copy-start | bytes 208900
  12.5 9.8 %collective-permute-start.2 = (f32[2,12,64]{2,1,0:T(8,128)S(1)}, f32[2,12,64]{2,1,0:T(8,128)S(1)}, u32[]{:S(2)}, u32[]{:S(2)}) collective-permute-start(f32[2,12,64]{2,1,0:T(8,128)S(1)} %get-tuple-element.63), channel_id=1, source_target_pairs={{0,240},{16,32},{32,16},{48,64},{64,48},{80,96},{96,80},{112,128},... | collective-permute-start | bytes 18440 | tf_op jit(solution)/shard_map/ppermute | solution.py:403
  17.6 4.8 %copy-start.8 = (f32[2,18,5000]{2,0,1:T(2,128)S(1)}, f32[2,18,5000]{2,0,1:T(2,128)}, u32[]{:S(2)}) copy-start(f32[2,18,5000]{2,0,1:T(2,128)} %param.16) | copy-start | bytes 2160004
  17.6 4.8 %collective-permute-start.3 = (f32[2,12,64]{2,1,0:T(8,128)S(1)}, f32[2,12,64]{2,1,0:T(8,128)S(1)}, u32[]{:S(2)}, u32[]{:S(2)}) collective-permute-start(f32[2,12,64]{2,1,0:T(8,128)S(1)} %get-tuple-element.62), channel_id=1, source_target_pairs={{0,16},{16,0},{32,48},{48,32},{64,80},{80,64},{96,112},{112,96},{1... | collective-permute-start | bytes 18440 | tf_op jit(solution)/shard_map/ppermute | solution.py:402
  22.7 6.9 %collective-permute-start.4 = (f32[8,12,2]{2,1,0:T(8,128)S(1)}, f32[8,12,2]{2,1,0:T(8,128)S(1)}, u32[]{:S(2)}, u32[]{:S(2)}) collective-permute-start(f32[8,12,2]{2,1,0:T(8,128)S(1)} %get-tuple-element.59), channel_id=1, source_target_pairs={{0,3},{1,2},{2,1},{3,0},{4,7},{5,6},{6,5},{7,4},{8,11},{9,10},{10,... | collective-permute-start | bytes 2312 | tf_op jit(solution)/shard_map/ppermute | solution.py:403
  24.5 5.2 %collective-permute-start.5 = (f32[8,12,2]{2,1,0:T(8,128)S(1)}, f32[8,12,2]{2,1,0:T(8,128)S(1)}, u32[]{:S(2)}, u32[]{:S(2)}) collective-permute-start(f32[8,12,2]{2,1,0:T(8,128)S(1)} %get-tuple-element.58), channel_id=1, source_target_pairs={{0,1},{1,0},{2,3},{3,2},{4,5},{5,4},{6,7},{7,6},{8,9},{9,8},{10,11... | collective-permute-start | bytes 2312 | tf_op jit(solution)/shard_map/ppermute | solution.py:402
